TPU v7x, 32 devices: a whole 2x2x4 slice. The times are simulated.
32 devices in a mesh: dp: 8 (over y, x, core), mp: 4 (over z).
Axes of the slice: x: 2, y: 2, z: 4, core: 2. Of those that a mesh axis runs over, the one named last changes fastest.
Arguments:
- frames: bfloat16 [8192, 1024], P(('dp', 'mp')), may hold values from -6 to 6
- lengths: int32 [8, 6], P('dp'), may hold values from 1 to 682, 896 in all within a row
- w_qkv: bfloat16 [3, 1024, 1024], P(None, None, 'mp'), may hold values from -0.1875 to 0.1875
- w_attn_out: bfloat16 [1024, 1024], P('mp'), may hold values from -0.5 to 0.5
- w_in: bfloat16 [1024, 4096], P(None, 'mp'), may hold values from -0.1875 to 0.1875
- w_out: bfloat16 [4096, 1024], P('mp'), may hold values from -0.09375 to 0.09375
- gain_attn: float32 [1024], replicated, may hold values from 0.5 to 1.5
- gain_mlp: float32 [1024], replicated, may hold values from 0.5 to 1.5
- cotangent: bfloat16 [8192, 1024], P(('dp', 'mp')), may hold values from -6 to 6
Outputs:
- output: bfloat16 [8192, 1024], P(('dp', 'mp'))
- grad_frames: float32 [8192, 1024], P(('dp', 'mp'))
- grad_w_qkv: float32 [3, 1024, 1024], P(None, None, 'mp')
- grad_w_attn_out: float32 [1024, 1024], P('mp')
- grad_w_in: float32 [1024, 4096], P(None, 'mp')
- grad_w_out: float32 [4096, 1024], P('mp')
- grad_gain_attn: float32 [1024], replicated
- grad_gain_mlp: float32 [1024], replicated
Inputs may be any that keep to these rules, and one draw needn't show every extreme that they name: `lengths`: each row holds the frame counts of the 6 items of one batch; they sum to 896 and the largest is exactly 682; the remaining frames of the batch are padding.
All inputs are finite; a program needn't handle non-finite values.
Results may differ from a plain program's by a relative error of at most 0.012.
Values may be sent and summed in bfloat16 or wider, within the bound.
A program may use at most 128 MiB of HBM per device.

v0:
```python
import jax
import jax.numpy as jnp
from jax import lax
from jax.sharding import PartitionSpec as P

HEAD = 64
BLOCK = 512


EPSILON = 1e-06
NEGATIVE = -1e30


def rms_scale(values, scaling_gain):
    return (
        values
        * lax.rsqrt(jnp.mean(values * values, axis=-1, keepdims=True) + EPSILON)
        * scaling_gain
    )


def gelu_tanh(values):
    return jax.nn.gelu(values, approximate=True)


def item_ids(length_row, frame_count):
    item_ends = jnp.cumsum(length_row)
    positions = jnp.arange(frame_count, dtype=jnp.int32)
    before = jnp.sum((positions[:, None] >= item_ends[None, :]).astype(jnp.int32), axis=1)
    return jnp.where(positions < item_ends[-1], before, before + positions + 1)


def block_scores(queries, positions, idents, keys_all, idents_all, scaling):
    scores = (
        jnp.einsum("bhd,khd->hbk", queries, keys_all, preferred_element_type=jnp.float32) * scaling
    )
    frame_count = keys_all.shape[0]
    visible = (idents[:, None] == idents_all[None, :]) & (
        jnp.arange(frame_count, dtype=jnp.int32)[None, :] <= positions[:, None]
    )
    return (scores, visible[None])


def per_device(frames, lengths, w_qkv, w_attn_out, w_in, w_out, gain_attn, gain_mlp, cotangent):
    frame_count = frames.shape[0] * lax.axis_size("mp")
    heads_here = w_attn_out.shape[0] // HEAD
    scaling = HEAD ** (-0.5)
    idents = item_ids(lengths[0], frame_count)
    positions = jnp.arange(frame_count, dtype=jnp.int32)
    frames_wide = frames.astype(jnp.float32)
    normed = rms_scale(frames_wide, gain_attn).astype(jnp.bfloat16)
    normed_all = lax.all_gather(normed, "mp", axis=0, tiled=True)
    projected = jnp.einsum(
        "td,cde->cte", normed_all, w_qkv, preferred_element_type=jnp.float32
    ).astype(jnp.bfloat16)
    head_split = projected.reshape(3, frame_count, heads_here, HEAD)
    queries, keys_all, values_all = (head_split[0], head_split[1], head_split[2])
    blocks = frame_count // BLOCK
    outputs = []
    log_totals = []
    for number in range(blocks):
        window = slice(number * BLOCK, (number + 1) * BLOCK)
        scores, visible = block_scores(
            queries[window], positions[window], idents[window], keys_all, idents, scaling
        )
        masked = jnp.where(visible, scores, NEGATIVE)
        row_peak = jnp.max(masked, axis=-1, keepdims=True)
        weights = jnp.where(visible, jnp.exp(masked - row_peak), 0.0)
        row_total = jnp.sum(weights, axis=-1, keepdims=True)
        probabilities = weights / row_total
        outputs.append(
            jnp.einsum(
                "hbk,khd->bhd",
                probabilities.astype(jnp.bfloat16),
                values_all,
                preferred_element_type=jnp.float32,
            )
        )
        log_totals.append(row_peak + jnp.log(row_total))
    attended = (
        jnp.concatenate(outputs, axis=0)
        .reshape(frame_count, heads_here * HEAD)
        .astype(jnp.bfloat16)
    )
    attn_part = jnp.dot(attended, w_attn_out, preferred_element_type=jnp.float32)
    attn_own = lax.psum_scatter(attn_part, "mp", scatter_dimension=0, tiled=True)
    resid = frames_wide + attn_own
    normed_mlp = rms_scale(resid, gain_mlp).astype(jnp.bfloat16)
    normed_mlp_all = lax.all_gather(normed_mlp, "mp", axis=0, tiled=True)
    hidden = jnp.dot(normed_mlp_all, w_in, preferred_element_type=jnp.float32)
    active = gelu_tanh(hidden).astype(jnp.bfloat16)
    mlp_own = lax.psum_scatter(
        jnp.dot(active, w_out, preferred_element_type=jnp.float32).astype(jnp.bfloat16),
        "mp",
        scatter_dimension=0,
        tiled=True,
    ).astype(jnp.float32)
    output = (resid + mlp_own).astype(jnp.bfloat16)
    grad_top = cotangent.astype(jnp.float32)
    grad_all = lax.all_gather(cotangent, "mp", axis=0, tiled=True)
    grad_w_out = jnp.einsum("tf,td->fd", active, grad_all, preferred_element_type=jnp.float32)
    grad_active = jnp.einsum("td,fd->tf", grad_all, w_out, preferred_element_type=jnp.float32)
    grad_hidden = jax.vjp(gelu_tanh, hidden)[1](grad_active)[0].astype(jnp.bfloat16)
    grad_w_in = jnp.einsum(
        "td,tf->df", normed_mlp_all, grad_hidden, preferred_element_type=jnp.float32
    )
    grad_normed_mlp = lax.psum_scatter(
        jnp.einsum("tf,df->td", grad_hidden, w_in, preferred_element_type=jnp.float32),
        "mp",
        scatter_dimension=0,
        tiled=True,
    )
    resid_back, gain_mlp_part = jax.vjp(rms_scale, resid, gain_mlp)[1](grad_normed_mlp)
    grad_resid = grad_top + resid_back
    grad_resid_all = lax.all_gather(grad_resid.astype(jnp.bfloat16), "mp", axis=0, tiled=True)
    grad_w_attn_out = jnp.einsum(
        "te,td->ed", attended, grad_resid_all, preferred_element_type=jnp.float32
    )
    grad_attended = (
        jnp.einsum("td,ed->te", grad_resid_all, w_attn_out, preferred_element_type=jnp.float32)
        .astype(jnp.bfloat16)
        .reshape(frame_count, heads_here, HEAD)
    )
    grad_keys = jnp.zeros((frame_count, heads_here, HEAD), jnp.float32)
    grad_values = jnp.zeros((frame_count, heads_here, HEAD), jnp.float32)
    grad_queries = []
    for number in range(blocks):
        window = slice(number * BLOCK, (number + 1) * BLOCK)
        scores, visible = block_scores(
            queries[window], positions[window], idents[window], keys_all, idents, scaling
        )
        probabilities = jnp.where(
            visible, jnp.exp(jnp.where(visible, scores, NEGATIVE) - log_totals[number]), 0.0
        )
        grad_rows = grad_attended[window]
        grad_probs = jnp.einsum(
            "bhd,khd->hbk", grad_rows, values_all, preferred_element_type=jnp.float32
        )
        grad_values = grad_values + jnp.einsum(
            "hbk,bhd->khd",
            probabilities.astype(jnp.bfloat16),
            grad_rows,
            preferred_element_type=jnp.float32,
        )
        inner_sum = jnp.sum(probabilities * grad_probs, axis=-1, keepdims=True)
        grad_scores = (probabilities * (grad_probs - inner_sum)).astype(jnp.bfloat16)
        grad_queries.append(
            jnp.einsum("hbk,khd->bhd", grad_scores, keys_all, preferred_element_type=jnp.float32)
            * scaling
        )
        grad_keys = (
            grad_keys
            + jnp.einsum(
                "hbk,bhd->khd", grad_scores, queries[window], preferred_element_type=jnp.float32
            )
            * scaling
        )
    grad_projected = jnp.stack(
        [
            jnp.concatenate(grad_queries, axis=0).reshape(frame_count, heads_here * HEAD),
            grad_keys.reshape(frame_count, heads_here * HEAD),
            grad_values.reshape(frame_count, heads_here * HEAD),
        ]
    ).astype(jnp.bfloat16)
    grad_w_qkv = jnp.einsum(
        "td,cte->cde", normed_all, grad_projected, preferred_element_type=jnp.float32
    )
    grad_normed = lax.psum_scatter(
        jnp.einsum("cte,cde->td", grad_projected, w_qkv, preferred_element_type=jnp.float32),
        "mp",
        scatter_dimension=0,
        tiled=True,
    )
    frames_back, gain_attn_part = jax.vjp(rms_scale, frames_wide, gain_attn)[1](grad_normed)
    grad_frames = grad_resid + frames_back
    grad_gain_attn, grad_gain_mlp = lax.psum((gain_attn_part, gain_mlp_part), ("dp", "mp"))
    grad_w_qkv, grad_w_attn_out, grad_w_in, grad_w_out = lax.psum(
        (grad_w_qkv, grad_w_attn_out, grad_w_in, grad_w_out), "dp"
    )
    return (
        output,
        grad_frames,
        grad_w_qkv,
        grad_w_attn_out,
        grad_w_in,
        grad_w_out,
        grad_gain_attn,
        grad_gain_mlp,
    )


def solution(mesh):
    in_specs = (
        P(("dp", "mp"), None),
        P("dp", None),
        P(None, None, "mp"),
        P("mp", None),
        P(None, "mp"),
        P("mp", None),
        P(),
        P(),
        P(("dp", "mp"), None),
    )
    out_specs = (
        P(("dp", "mp"), None),
        P(("dp", "mp"), None),
        P(None, None, "mp"),
        P("mp", None),
        P(None, "mp"),
        P("mp", None),
        P(),
        P(),
    )
    return jax.shard_map(
        per_device, mesh=mesh, in_specs=in_specs, out_specs=out_specs, check_vma=False
    )
```

profile of v0, /device:TPU:0, one launch (start us, length us, event | category | flops | bytes accessed | tf_op | source)
XLA Modules:
  0.0 765.3 jit_solution(12484631126287785952)
XLA Ops:
  8.6 2.0 fusion.50
  12.9 1.8 fusion.21
  14.7 44.8 %all-gather.5.cloned.1.call-done = bf16[1024,1024]{1,0:T(8,128)(2,1)} async-done(((bf16[256,1024]{1,0:T(8,128)(2,1)}), bf16[1024,1024]{1,0:T(8,128)(2,1)}) %all-gather.5.cloned.1.call-update) | async-done | bytes 2097168 | tf_op jit(solution)/shard_map/all_gather | solution.py:52
  59.5 3.9 fusion.29
  63.6 1.7 fusion.3
  65.2 2.9 fusion.1
  68.5 3.3 fusion.47
  71.8 1.7 fusion.2
  73.5 2.9 fusion
  76.8 3.3 fusion.46
  80.2 2.8 fusion.78
  84.0 74.6 %reduce-scatter.5.cloned.1.call-done = f32[256,1024]{1,0:T(8,128)} async-done(((f32[1024,1024]{1,0:T(8,128)}), f32[256,1024]{1,0:T(8,128)}) %reduce-scatter.5.cloned.1.call-update) | async-done | bytes 1048592 | tf_op jit(solution)/shard_map/reduce_scatter | solution.py:86
  158.6 1.6 multiply_reduce_fusion.4
  161.2 45.5 %all-gather.9.cloned.1.call-done = bf16[1024,1024]{1,0:T(8,128)(2,1)} async-done(((bf16[256,1024]{1,0:T(8,128)(2,1)}), bf16[1024,1024]{1,0:T(8,128)(2,1)}) %all-gather.9.cloned.1.call-update) | async-done | bytes 2097168 | tf_op jit(solution)/shard_map/all_gather | solution.py:100
  206.8 6.6 fusion.79
  213.4 40.2 %all-gather.7.cloned.1.call-done = bf16[1024,1024]{1,0:T(8,128)(2,1)} async-done(((bf16[256,1024]{1,0:T(8,128)(2,1)}), bf16[1024,1024]{1,0:T(8,128)(2,1)}) %all-gather.7.cloned.1.call-update) | async-done | bytes 2097168 | tf_op jit(solution)/shard_map/all_gather | solution.py:89
  253.5 8.2 %fusion.10 = (bf16[1024,1024]{1,0:T(8,128)(2,1)S(1)}, f32[1024,1024]{1,0:T(8,128)}) fusion(f32[1024,1024]{1,0:T(8,128)} %fusion.79, bf16[1024,1024]{1,0:T(8,128)(2,1)} %all-gather.7.cloned.1.call-done, bf16[1024,1024]{1,0:T(8,128)(2,1)S(1)} %copy-done), kind=kOutput, calls=%fused_computation.24 | convolution fusion | flops 2168455168 | bytes 14680064 | tf_op jit(solution)/shard_map/dot_general | solution.py:90
  263.1 4.4 fusion.80
  267.6 75.6 %reduce-scatter.9.cloned.1.call-done = f32[256,1024]{1,0:T(8,128)} async-done(((f32[1024,1024]{1,0:T(8,128)}), f32[256,1024]{1,0:T(8,128)}) %reduce-scatter.9.cloned.1.call-update) | async-done | bytes 1048592 | tf_op jit(solution)/shard_map/reduce_scatter | solution.py:107
  343.2 1.5 multiply_reduce_fusion.2
  344.7 2.3 fusion.72
  347.6 6.7 fusion.83
  354.3 4.8 fusion.73
  359.1 34.6 %all-gather.11.cloned.1.call-done = bf16[1024,1024]{1,0:T(8,128)(2,1)} async-done(((bf16[256,1024]{1,0:T(8,128)(2,1)}), bf16[1024,1024]{1,0:T(8,128)(2,1)}) %all-gather.11.cloned.1.call-update) | async-done | bytes 2097168 | tf_op jit(solution)/shard_map/all_gather | solution.py:115
  393.6 2.5 convolution_convert_fusion.1
  396.2 5.2 fusion.11
  401.4 5.7 multiply_reduce_fusion
  407.2 5.8 multiply_reduce_fusion.1
  413.0 10.4 %multiply_convert_fusion = (bf16[4,512,1024]{2,1,0:T(8,128)(2,1)}, bf16[4,512,1024]{2,1,0:T(8,128)(2,1)S(1)}) fusion(f32[4,512,1024]{2,1,0:T(8,128)} %get-tuple-element.57, f32[4,512]{1,0:T(4,128)S(1)} %get-tuple-element.56, f32[4,512]{1,0:T(4,128)S(1)} %log_add_fusion, f32[4,512,1024]{2,1,0:T(8,128)S(1)} %bitcast.83, pred[512,1024]{1,0:T(8,128)(4,1)S(1)} %copy-done.12, ...), kind=kLoop, calls=%fused_computation | loop fusion | flops 29360128 | bytes 43024384 | tf_op jit(solution)/shard_map/convert_element_type | solution.py:146
  423.5 2.1 fusion.49
  426.4 3.3 fusion.36
  429.7 2.0 copy.26
  431.8 4.4 fusion.48
  440.3 3.3 fusion.82
  443.5 5.3 fusion.23
  449.9 5.2 convolution_bitcast_fusion
  455.2 1.5 copy-done.31
  456.7 6.3 convolution_convert_fusion
  463.0 158.1 %all-reduce.4.cloned.1.call-done = (f32[3,1024,256]{1,2,0:T(8,128)}, f32[256,1024]{1,0:T(8,128)}, f32[1024,1024]{1,0:T(8,128)}, f32[1024,1024]{1,0:T(8,128)}) async-done(((f32[3,1024,256]{1,2,0:T(8,128)}, f32[256,1024]{1,0:T(8,128)}, f32[1024,1024]{1,0:T(8,128)}, f32[1024,1024]{1,0:T(8,128)}), (f32[3,1024,256]{1,2,0:T(8,128)}, f32[256,1024]{1,0:T(8,128)}, f32[1024,1024]{1,0:T(8,128)}, ...) | async-done | bytes 12582928 | tf_op jit(solution)/shard_map/psum | solution.py:177
  621.1 3.5 copy.28
  624.7 76.3 %reduce-scatter.11.cloned.1.call-done = f32[256,1024]{1,0:T(8,128)} async-done(((f32[1024,1024]{1,0:T(8,128)}), f32[256,1024]{1,0:T(8,128)}) %reduce-scatter.11.cloned.1.call-update) | async-done | bytes 1048592 | tf_op jit(solution)/shard_map/reduce_scatter | solution.py:168
  701.0 1.6 fusion.51
  702.6 43.7 %all-reduce = (f32[1024]{0:T(1024)}, f32[1024]{0:T(1024)}) all-reduce(f32[1024]{0:T(1024)S(1)} %get-tuple-element.26, f32[1024]{0:T(1024)S(1)} %get-tuple-element.24), channel_id=1, replica_groups=mesh['dp'=8,'mp'=4] {'dp','mp'}, use_global_device_ids=true, to_apply=%region_21.22 | all-reduce | flops 2048 | bytes 16384 | tf_op jit(solution)/shard_map/psum | solution.py:176
  746.3 2.4 reduce-scatter.7.cloned.1.call-done
  748.7 3.2 fusion.53
  752.9 2.1 copy.36
  755.0 1.6 copy-done.17
  756.6 2.0 copy.37
  (123 shorter events, 15.5 us)
Async XLA Ops:
  7.2 246.4 %copy-start = (bf16[1024,1024]{1,0:T(8,128)(2,1)S(1)}, bf16[1024,1024]{1,0:T(8,128)(2,1)}, u32[]{:S(2)}) copy-start(bf16[1024,1024]{1,0:T(8,128)(2,1)} %param.13) | copy-start | bytes 6291460
  7.2 52.3 %all-gather.5.cloned.1.call-start = ((), (), s32[]{:S(2)}) async-start(), calls=%async_computation.4 | async-start | bytes 2621440 | tf_op jit(solution)/shard_map/all_gather | solution.py:52
  10.7 148.0 %reduce-scatter.5.cloned.1.call-start = ((), (), s32[]{:S(2)}) async-start(), calls=%async_computation.5 | async-start | bytes 5242880 | tf_op jit(solution)/shard_map/reduce_scatter | solution.py:86
  14.7 61.8 %copy-start.9 = (pred[512,1024]{1,0:T(8,128)(4,1)}, pred[512,1024]{1,0:T(8,128)(4,1)S(1)}, u32[]{:S(2)}) copy-start(pred[512,1024]{1,0:T(8,128)(4,1)S(1)} %get-tuple-element.44) | copy-start | bytes 1572868
  59.5 4.1 copy-start.11
  63.4 8.4 %copy-start.19 = (bf16[1,512,256]{1,2,0:T(8,128)(2,1)}, bf16[1,512,256]{1,2,0:T(8,128)(2,1)S(1)}, u32[]{:S(2)}) copy-start(bf16[1,512,256]{1,2,0:T(8,128)(2,1)S(1)} %get-tuple-element.36) | copy-start | bytes 786436
  63.5 8.3 %copy-start.5 = (bf16[1,1024,256]{1,2,0:T(8,128)(2,1)}, bf16[1,1024,256]{1,2,0:T(8,128)(2,1)S(1)}, u32[]{:S(2)}) copy-start(bf16[1,1024,256]{1,2,0:T(8,128)(2,1)S(1)} %get-tuple-element.38) | copy-start | bytes 1572868
  63.5 12.9 %copy-start.27 = (bf16[1,1024,256]{1,2,0:T(8,128)(2,1)}, bf16[1,1024,256]{1,2,0:T(8,128)(2,1)S(1)}, u32[]{:S(2)}) copy-start(bf16[1,1024,256]{1,2,0:T(8,128)(2,1)S(1)} %get-tuple-element.39) | copy-start | bytes 1572868
  65.2 3.2 copy-start.3
  73.5 3.3 copy-start.2
  76.8 3.4 copy-start.22
  80.2 2.8 copy-start.13
  83.0 77.2 %copy-start.29 = (f32[1024]{0:T(1024)S(1)}, f32[1024]{0:T(1024)}, u32[]{:S(2)}) copy-start(f32[1024]{0:T(1024)} %param.16) | copy-start | bytes 12292
  83.0 123.8 %all-gather.9.cloned.1.call-start = ((), (), s32[]{:S(2)}) async-start(), calls=%async_computation.8 | async-start | bytes 2621440 | tf_op jit(solution)/shard_map/all_gather | solution.py:100
  83.7 169.8 %all-gather.7.cloned.1.call-start = ((), (), s32[]{:S(2)}) async-start(), calls=%async_computation.6 | async-start | bytes 2621440 | tf_op jit(solution)/shard_map/all_gather | solution.py:89
  161.2 182.0 %reduce-scatter.9.cloned.1.call-start = ((), (), s32[]{:S(2)}) async-start(), calls=%async_computation.9 | async-start | bytes 5242880 | tf_op jit(solution)/shard_map/reduce_scatter | solution.py:107
  261.8 1.3 copy-start.33
  267.5 77.1 %copy-start.15 = (bf16[256,1024]{1,0:T(8,128)(2,1)S(1)}, bf16[256,1024]{1,0:T(8,128)(2,1)}, u32[]{:S(2)}) copy-start(bf16[256,1024]{1,0:T(8,128)(2,1)} %param.17) | copy-start | bytes 1572868
  267.6 126.1 %all-gather.11.cloned.1.call-start = ((), (), s32[]{:S(2)}) async-start(), calls=%async_computation.10 | async-start | bytes 2621440 | tf_op jit(solution)/shard_map/all_gather | solution.py:115
  347.0 274.1 %all-reduce.4.cloned.1.call-start = ((), (), s32[]{:S(2)}) async-start(), calls=%async_computation.12 | async-start | bytes 25165824 | tf_op jit(solution)/shard_map/psum | solution.py:177
  347.5 6.7 copy-start.32
  347.5 6.7 copy-start.34
  354.3 39.4 %copy-start.23 = (bf16[256,1024]{1,0:T(8,128)(2,1)S(1)}, bf16[256,1024]{1,0:T(8,128)(2,1)}, u32[]{:S(2)}) copy-start(bf16[256,1024]{1,0:T(8,128)(2,1)} %param.12) | copy-start | bytes 1572868
  359.1 37.1 %copy-start.12 = (pred[512,1024]{1,0:T(8,128)(4,1)S(1)}, pred[512,1024]{1,0:T(8,128)(4,1)}, u32[]{:S(2)}) copy-start(pred[512,1024]{1,0:T(8,128)(4,1)} %get-tuple-element.45) | copy-start | bytes 1572868
  393.6 7.7 %slice-start.2 = ((s8[8388608]{0:T(1024)(128)(4,1)}), s8[4194304]{0:T(1024)(128)(4,1)S(1)}, s32[]{:S(2)}) async-start(s8[8388608]{0:T(1024)(128)(4,1)} %bitcast.82), calls=%async_computation.15 | async-start | bytes 8388608
  396.2 5.2 slice-start.3
  396.2 5.2 copy-start.28
  396.2 11.0 %slice-start = ((s8[8388608]{0:T(1024)(128)(4,1)}), s8[4194304]{0:T(1024)(128)(4,1)S(1)}, s32[]{:S(2)}) async-start(s8[8388608]{0:T(1024)(128)(4,1)} %bitcast.80), calls=%async_computation.13 | async-start | bytes 8388608
  401.4 5.8 slice-start.1
  401.4 5.8 copy-start.10
  413.0 10.5 %copy-start.6 = (bf16[1,1024,256]{1,2,0:T(8,128)(2,1)S(1)}, bf16[1,1024,256]{1,2,0:T(8,128)(2,1)}, u32[]{:S(2)}) copy-start(bf16[1,1024,256]{1,2,0:T(8,128)(2,1)} %copy-done.5) | copy-start | bytes 1572868
  423.5 2.1 copy-start.20
  431.8 4.4 copy-start.4
  436.2 4.1 copy-start.14
  437.1 6.4 copy-start.24
  438.1 5.4 copy-start.25
  448.8 1.0 copy-start.26
  448.9 252.1 %reduce-scatter.11.cloned.1.call-start = ((), (), s32[]{:S(2)}) async-start(), calls=%async_computation.11 | async-start | bytes 5242880 | tf_op jit(solution)/shard_map/reduce_scatter | solution.py:168
  455.1 1.6 copy-start.31
  455.1 293.6 %reduce-scatter.7.cloned.1.call-start = ((), (), s32[]{:S(2)}) async-start(), calls=%async_computation.7 | async-start | bytes 2621440 | tf_op jit(solution)/shard_map/reduce_scatter | solution.py:92
  463.0 238.0 %copy-start.7 = (bf16[256,1024]{1,0:T(8,128)(2,1)S(1)}, bf16[256,1024]{1,0:T(8,128)(2,1)}, u32[]{:S(2)}) copy-start(bf16[256,1024]{1,0:T(8,128)(2,1)} %param.9) | copy-start | bytes 1572868
  463.0 238.0 %copy-start.30 = (f32[1024]{0:T(1024)S(1)}, f32[1024]{0:T(1024)}, u32[]{:S(2)}) copy-start(f32[1024]{0:T(1024)} %param.15) | copy-start | bytes 12292
  463.0 285.7 %copy-start.8 = (f32[256,1024]{1,0:T(8,128)S(1)}, f32[256,1024]{1,0:T(8,128)}, u32[]{:S(2)}) copy-start(f32[256,1024]{1,0:T(8,128)} %reduce-scatter.9.cloned.1.call-done) | copy-start | bytes 3145732
  463.0 285.7 %copy-start.16 = (bf16[256,1024]{1,0:T(8,128)(2,1)S(1)}, bf16[256,1024]{1,0:T(8,128)(2,1)}, u32[]{:S(2)}) copy-start(bf16[256,1024]{1,0:T(8,128)(2,1)} %param.17) | copy-start | bytes 1572868
  748.7 3.2 copy-start.21
  748.7 4.2 copy-start.18
  752.9 3.7 copy-start.17
  752.9 5.7 copy-start.1
Sparse Core Ops, SparseCore 0:
  10.8 48.6 all-gather.4
  83.1 75.4 reduce-scatter.4
  160.3 46.4 all-gather.8
  208.8 44.6 all-gather.6
  267.7 75.4 reduce-scatter.8
  347.2 46.4 all-gather.10
  449.0 172.0 all-reduce.3
  624.1 76.8 reduce-scatter.10
  703.3 45.3 reduce-scatter.6
where the time goes:
time: 774 us; the launch traced here: 765 us
  waiting for transfers between devices  553 us (71%)
  matrix products  98.3 us (13%)
  blocking collectives  43.7 us (6%)
  other arithmetic  35.3 us (5%)
  local copies, waits for them, and re-layouts  19.6 us (3%)
  between operations  14.5 us (2%)
    psum x1, waiting for transfers between devices, per_device(): lax.psum((grad_w_qkv, grad_w_attn_out, grad_w_in, grad_w_out), 'dp')  158 us
    reduce_scatter x1, waiting for transfers between devices, per_device(): lax.psum_scatter(jnp.einsum('cte,cde->td', grad_projected, w_qkv, preferr...  76.3 us
    reduce_scatter x1, waiting for transfers between devices, per_device(): lax.psum_scatter(jnp.einsum('tf,df->td', grad_hidden, w_in, preferred_ele...  75.6 us
    reduce_scatter x1, waiting for transfers between devices, per_device(): lax.psum_scatter(attn_part, 'mp', scatter_dimension=0, tiled=True)  74.6 us
    all_gather x1, waiting for transfers between devices, per_device(): grad_all = lax.all_gather(cotangent, 'mp', axis=0, tiled=True)  45.5 us
    all_gather x1, waiting for transfers between devices, per_device(): normed_all = lax.all_gather(normed, 'mp', axis=0, tiled=True)  44.8 us
    psum x1, blocking collectives, per_device(): lax.psum((gain_attn_part, gain_mlp_part), ('dp', 'mp'))  43.7 us
    all_gather x1, waiting for transfers between devices, per_device(): normed_mlp_all = lax.all_gather(normed_mlp, 'mp', axis=0, tiled=True)  40.2 us
  transfers between devices with their start and end apart: 9, of which 9 were waited for; matrix products, arithmetic and copies ran while one was open for 5% of the time, Pallas kernels for 0%

commit v1 on v0

--- a/solution.py
+++ b/solution.py
@@ -39,6 +39,17 @@
         jnp.arange(frame_count, dtype=jnp.int32)[None, :] <= positions[:, None]
     )
     return (scores, visible[None])
+
+
+def scatter_sum(part):
+    return lax.psum_scatter(
+        part.astype(jnp.bfloat16), "mp", scatter_dimension=0, tiled=True
+    ).astype(jnp.float32)
+
+
+def batch_sum(parts):
+    sent = tuple(part.astype(jnp.bfloat16) for part in parts)
+    return tuple(total.astype(jnp.float32) for total in lax.psum(sent, "dp"))
 
 
 def per_device(frames, lengths, w_qkv, w_attn_out, w_in, w_out, gain_attn, gain_mlp, cotangent):
@@ -83,7 +94,7 @@
         .astype(jnp.bfloat16)
     )
     attn_part = jnp.dot(attended, w_attn_out, preferred_element_type=jnp.float32)
-    attn_own = lax.psum_scatter(attn_part, "mp", scatter_dimension=0, tiled=True)
+    attn_own = scatter_sum(attn_part)
     resid = frames_wide + attn_own
     normed_mlp = rms_scale(resid, gain_mlp).astype(jnp.bfloat16)
     normed_mlp_all = lax.all_gather(normed_mlp, "mp", axis=0, tiled=True)
@@ -104,11 +115,8 @@
     grad_w_in = jnp.einsum(
         "td,tf->df", normed_mlp_all, grad_hidden, preferred_element_type=jnp.float32
     )
-    grad_normed_mlp = lax.psum_scatter(
-        jnp.einsum("tf,df->td", grad_hidden, w_in, preferred_element_type=jnp.float32),
-        "mp",
-        scatter_dimension=0,
-        tiled=True,
+    grad_normed_mlp = scatter_sum(
+        jnp.einsum("tf,df->td", grad_hidden, w_in, preferred_element_type=jnp.float32)
     )
     resid_back, gain_mlp_part = jax.vjp(rms_scale, resid, gain_mlp)[1](grad_normed_mlp)
     grad_resid = grad_top + resid_back
@@ -165,18 +173,14 @@
     grad_w_qkv = jnp.einsum(
         "td,cte->cde", normed_all, grad_projected, preferred_element_type=jnp.float32
     )
-    grad_normed = lax.psum_scatter(
-        jnp.einsum("cte,cde->td", grad_projected, w_qkv, preferred_element_type=jnp.float32),
-        "mp",
-        scatter_dimension=0,
-        tiled=True,
+    grad_normed = scatter_sum(
+        jnp.einsum("cte,cde->td", grad_projected, w_qkv, preferred_element_type=jnp.float32)
     )
     frames_back, gain_attn_part = jax.vjp(rms_scale, frames_wide, gain_attn)[1](grad_normed)
     grad_frames = grad_resid + frames_back
     grad_gain_attn, grad_gain_mlp = lax.psum((gain_attn_part, gain_mlp_part), ("dp", "mp"))
-    grad_w_qkv, grad_w_attn_out, grad_w_in, grad_w_out = lax.psum(
-        (grad_w_qkv, grad_w_attn_out, grad_w_in, grad_w_out), "dp"
-    )
+    grad_w_in, grad_w_out = batch_sum((grad_w_in, grad_w_out))
+    grad_w_qkv, grad_w_attn_out = batch_sum((grad_w_qkv, grad_w_attn_out))
     return (
         output,
         grad_frames,

time: 774 us -> 590 us (0.76)
  waiting for transfers between devices: 553 us -> 378 us
  local copies, waits for them, and re-layouts: 19.6 us -> 8.28 us
    reduce_scatter x3, waiting for transfers between devices: 227 us -> 120 us  [scatter_sum(): lax.psum_scatter(part.astype(jnp.bfloat16), 'mp', scatter_dimension=0, ti...]
    psum x1, waiting for transfers between devices: 158 us -> 91.6 us  [batch_sum(): return tuple((total.astype(jnp.float32) for total in lax.psum(sent, 'dp')))]
    unnamed x82 -> x65, local copies, waits for them, and re-layouts: 14.8 us -> 6.12 us
  transfers between devices with their start and end apart: 9 -> 9, of which waited for: 9 -> 9; matrix products, arithmetic and copies ran while one was open for 5% -> 8% of each run, Pallas kernels for 0% -> 0%
where the time goes in v1:
time: 590 us; the launch traced here: 581 us
  waiting for transfers between devices  378 us (64%)
  matrix products  93.5 us (16%)
  other arithmetic  42.8 us (7%)
  blocking collectives  42.6 us (7%)
  between operations  14.5 us (2%)
  local copies, waits for them, and re-layouts  8.28 us (1%)
    reduce_scatter x3, waiting for transfers between devices, scatter_sum(): lax.psum_scatter(part.astype(jnp.bfloat16), 'mp', scatter_dimension=0, ti...  120 us
    psum x1, waiting for transfers between devices, batch_sum(): return tuple((total.astype(jnp.float32) for total in lax.psum(sent, 'dp')))  91.6 us
    all_gather x1, waiting for transfers between devices, per_device(): normed_all = lax.all_gather(normed, 'mp', axis=0, tiled=True)  44.8 us
    all_gather x1, waiting for transfers between devices, per_device(): grad_all = lax.all_gather(cotangent, 'mp', axis=0, tiled=True)  43.5 us
    psum x1, blocking collectives, per_device(): lax.psum((gain_attn_part, gain_mlp_part), ('dp', 'mp'))  42.6 us
    all_gather x1, waiting for transfers between devices, per_device(): normed_mlp_all = lax.all_gather(normed_mlp, 'mp', axis=0, tiled=True)  40.2 us
    all_gather x1, waiting for transfers between devices, per_device(): lax.all_gather(grad_resid.astype(jnp.bfloat16), 'mp', axis=0, tiled=True)  34.7 us
  transfers between devices with their start and end apart: 9, of which 9 were waited for; matrix products, arithmetic and copies ran while one was open for 8% of the time, Pallas kernels for 0%

profile of v1, /device:TPU:0, one launch (start us, length us, event | category | flops | bytes accessed | tf_op | source)
XLA Modules:
  0.0 581.1 jit_solution(17814917532869155465)
XLA Ops:
  7.2 1.4 fusion.61
  8.6 2.0 fusion.55
  12.9 1.8 fusion.21
  14.7 44.8 %all-gather.5.cloned.1.call-done = bf16[1024,1024]{1,0:T(8,128)(2,1)} async-done(((bf16[256,1024]{1,0:T(8,128)(2,1)}), bf16[1024,1024]{1,0:T(8,128)(2,1)}) %all-gather.5.cloned.1.call-update) | async-done | bytes 2097168 | tf_op jit(solution)/shard_map/all_gather | solution.py:63
  59.5 3.9 fusion.32
  63.5 1.7 fusion.3
  65.2 2.9 fusion.1
  68.5 3.3 fusion.52
  71.8 1.7 fusion.2
  73.5 2.9 fusion
  76.7 3.3 fusion.51
  80.9 2.1 convolution_convert_fusion.4
  84.0 41.8 %reduce-scatter.5.cloned.1.call-done = bf16[256,1024]{1,0:T(8,128)(2,1)} async-done(((bf16[1024,1024]{1,0:T(8,128)(2,1)}), bf16[256,1024]{1,0:T(8,128)(2,1)}) %reduce-scatter.5.cloned.1.call-update) | async-done | bytes 524304 | tf_op jit(solution)/shard_map/reduce_scatter | solution.py:45
  127.1 2.0 multiply_convert_fusion.3
  129.2 43.5 %all-gather.9.cloned.1.call-done = bf16[1024,1024]{1,0:T(8,128)(2,1)} async-done(((bf16[256,1024]{1,0:T(8,128)(2,1)}), bf16[1024,1024]{1,0:T(8,128)(2,1)}) %all-gather.9.cloned.1.call-update) | async-done | bytes 2097168 | tf_op jit(solution)/shard_map/all_gather | solution.py:111
  172.7 6.6 %fusion.84 = f32[1024,1024]{1,0:T(8,128)} fusion(bf16[1024,1024]{1,0:T(8,128)(2,1)} %all-gather.9.cloned.1.call-done, bf16[1024,1024]{1,0:T(8,128)(2,1)} %param.14), kind=kOutput, calls=%fused_computation.127 | convolution fusion | flops 2147483648 | bytes 8388608 | tf_op jit(solution)/shard_map/td,fd->tf/dot_general | solution.py:113
  179.3 40.2 %all-gather.7.cloned.1.call-done = bf16[1024,1024]{1,0:T(8,128)(2,1)} async-done(((bf16[256,1024]{1,0:T(8,128)(2,1)}), bf16[1024,1024]{1,0:T(8,128)(2,1)}) %all-gather.7.cloned.1.call-update) | async-done | bytes 2097168 | tf_op jit(solution)/shard_map/all_gather | solution.py:100
  219.5 8.2 %fusion.10 = (bf16[1024,1024]{1,0:T(8,128)(2,1)S(1)}, f32[1024,1024]{1,0:T(8,128)}) fusion(f32[1024,1024]{1,0:T(8,128)} %fusion.84, bf16[1024,1024]{1,0:T(8,128)(2,1)} %all-gather.7.cloned.1.call-done, bf16[1024,1024]{1,0:T(8,128)(2,1)S(1)} %copy-done), kind=kOutput, calls=%fused_computation.24 | convolution fusion | flops 2168455168 | bytes 14680064 | tf_op jit(solution)/shard_map/dot_general | solution.py:101
  227.7 1.3 copy-done.27
  229.0 3.8 convolution_convert_fusion.2
  232.9 42.7 %reduce-scatter.9.cloned.1.call-done = bf16[256,1024]{1,0:T(8,128)(2,1)} async-done(((bf16[1024,1024]{1,0:T(8,128)(2,1)}), bf16[256,1024]{1,0:T(8,128)(2,1)}) %reduce-scatter.9.cloned.1.call-update) | async-done | bytes 524304 | tf_op jit(solution)/shard_map/reduce_scatter | solution.py:45
  275.6 1.7 fusion.57
  277.3 2.6 fusion.79
  280.4 6.1 %convolution_convert_fusion.1 = bf16[1024,1024]{1,0:T(8,128)(2,1)} fusion(bf16[1024,1024]{1,0:T(8,128)(2,1)} %all-gather.7.cloned.1.call-done, bf16[1024,1024]{1,0:T(8,128)(2,1)} %copy-done.27), kind=kOutput, calls=%fused_computation.47 | convolution fusion | flops 2148532224 | bytes 6291456 | tf_op jit(solution)/shard_map/td,tf->df/dot_general | solution.py:115
  286.4 4.1 convolution_convert_fusion
  290.5 34.7 %all-gather.11.cloned.1.call-done = bf16[1024,1024]{1,0:T(8,128)(2,1)} async-done(((bf16[256,1024]{1,0:T(8,128)(2,1)}), bf16[1024,1024]{1,0:T(8,128)(2,1)}) %all-gather.11.cloned.1.call-update) | async-done | bytes 2097168 | tf_op jit(solution)/shard_map/all_gather | solution.py:123
  325.2 2.5 convolution_convert_fusion.6
  327.8 5.1 fusion.11
  333.0 5.7 multiply_reduce_fusion
  338.8 5.8 multiply_reduce_fusion.1
  344.5 10.4 %multiply_convert_fusion = (bf16[4,512,1024]{2,1,0:T(8,128)(2,1)}, bf16[4,512,1024]{2,1,0:T(8,128)(2,1)S(1)}) fusion(f32[4,512,1024]{2,1,0:T(8,128)} %get-tuple-element.55, f32[4,512]{1,0:T(4,128)S(1)} %get-tuple-element.54, f32[4,512]{1,0:T(4,128)S(1)} %log_add_fusion, f32[4,512,1024]{2,1,0:T(8,128)S(1)} %bitcast.85, pred[512,1024]{1,0:T(8,128)(4,1)S(1)} %copy-done.10, ...), kind=kLoop, calls=%fused_computation | loop fusion | flops 29360128 | bytes 43024384 | tf_op jit(solution)/shard_map/convert_element_type | solution.py:154
  354.9 2.1 fusion.54
  357.9 2.5 fusion.39
  361.4 3.7 fusion.53
  366.6 3.1 convolution_convert_fusion.5
  369.7 4.6 fusion.29
  374.3 4.6 bitcast_convert_fusion
  379.0 7.3 %convolution_convert_fusion.3 = bf16[1024,1024]{1,0:T(8,128)(2,1)} fusion(bf16[1024,1024]{1,0:T(8,128)(2,1)} %param.14, f32[1024,1024]{1,0:T(8,128)} %get-tuple-element.51), kind=kOutput, calls=%fused_computation.49 | convolution fusion | flops 2157969408 | bytes 8388608 | tf_op jit(solution)/shard_map/dot_general | solution.py:104
  386.3 91.6 %all-reduce.4.cloned.1.call-done = (bf16[3,1024,256]{1,2,0:T(8,128)(2,1)}, bf16[256,1024]{1,0:T(8,128)(2,1)}, bf16[1024,1024]{1,0:T(8,128)(2,1)}, bf16[1024,1024]{1,0:T(8,128)(2,1)}) async-done(((bf16[3,1024,256]{1,2,0:T(8,128)(2,1)}, bf16[256,1024]{1,0:T(8,128)(2,1)}, bf16[1024,1024]{1,0:T(8,128)(2,1)}, bf16[1024,1024]{1,0:T(8,128)(2,1)}), (bf16[3,1024,256]{1,2,0:T(8,128)(2,1)}, ...) | async-done | bytes 6291472 | tf_op jit(solution)/shard_map/psum | solution.py:52
  477.9 2.3 convert_element_type.141
  480.2 3.3 copy.28
  483.5 2.5 convert_element_type.143
  486.0 2.5 convert_element_type.145
  488.5 35.9 %reduce-scatter.11.cloned.1.call-done = bf16[256,1024]{1,0:T(8,128)(2,1)} async-done(((bf16[1024,1024]{1,0:T(8,128)(2,1)}), bf16[256,1024]{1,0:T(8,128)(2,1)}) %reduce-scatter.11.cloned.1.call-update) | async-done | bytes 524304 | tf_op jit(solution)/shard_map/reduce_scatter | solution.py:45
  524.3 1.5 fusion.58
  525.8 42.6 %all-reduce = (f32[1024]{0:T(1024)}, f32[1024]{0:T(1024)}) all-reduce(f32[1024]{0:T(1024)S(1)} %get-tuple-element.26, f32[1024]{0:T(1024)S(1)} %get-tuple-element.24), channel_id=1, replica_groups=mesh['dp'=8,'mp'=4] {'dp','mp'}, use_global_device_ids=true, to_apply=%region_21.22 | all-reduce | flops 2048 | bytes 16384 | tf_op jit(solution)/shard_map/psum | solution.py:181
  568.5 2.4 reduce-scatter.7.cloned.1.call-done
  570.9 3.4 fusion.60
  (109 shorter events, 10.3 us)
Async XLA Ops:
  7.2 212.3 %copy-start = (bf16[1024,1024]{1,0:T(8,128)(2,1)S(1)}, bf16[1024,1024]{1,0:T(8,128)(2,1)}, u32[]{:S(2)}) copy-start(bf16[1024,1024]{1,0:T(8,128)(2,1)} %param.13) | copy-start | bytes 6291460
  7.2 52.3 %all-gather.5.cloned.1.call-start = ((), (), s32[]{:S(2)}) async-start(), calls=%async_computation.4 | async-start | bytes 2621440 | tf_op jit(solution)/shard_map/all_gather | solution.py:63
  10.7 115.1 %reduce-scatter.5.cloned.1.call-start = ((), (), s32[]{:S(2)}) async-start(), calls=%async_computation.5 | async-start | bytes 2621440 | tf_op jit(solution)/shard_map/reduce_scatter | solution.py:45
  14.7 61.7 %copy-start.7 = (pred[512,1024]{1,0:T(8,128)(4,1)}, pred[512,1024]{1,0:T(8,128)(4,1)S(1)}, u32[]{:S(2)}) copy-start(pred[512,1024]{1,0:T(8,128)(4,1)S(1)} %get-tuple-element.42) | copy-start | bytes 1572868
  59.5 4.1 copy-start.9
  63.4 8.4 %copy-start.11 = (bf16[1,512,256]{1,2,0:T(8,128)(2,1)}, bf16[1,512,256]{1,2,0:T(8,128)(2,1)S(1)}, u32[]{:S(2)}) copy-start(bf16[1,512,256]{1,2,0:T(8,128)(2,1)S(1)} %get-tuple-element.34) | copy-start | bytes 786436
  63.5 12.9 %copy-start.21 = (bf16[1,1024,256]{1,2,0:T(8,128)(2,1)}, bf16[1,1024,256]{1,2,0:T(8,128)(2,1)S(1)}, u32[]{:S(2)}) copy-start(bf16[1,1024,256]{1,2,0:T(8,128)(2,1)S(1)} %get-tuple-element.37) | copy-start | bytes 1572868
  65.2 3.2 copy-start.3
  73.5 3.2 copy-start.2
  76.7 4.2 copy-start.19
  80.1 45.7 %copy-start.5 = (bf16[256,1024]{1,0:T(8,128)(2,1)S(1)}, bf16[256,1024]{1,0:T(8,128)(2,1)}, u32[]{:S(2)}) copy-start(bf16[256,1024]{1,0:T(8,128)(2,1)} %param.9) | copy-start | bytes 1572868
  80.1 47.0 %copy-start.23 = (f32[1024]{0:T(1024)S(1)}, f32[1024]{0:T(1024)}, u32[]{:S(2)}) copy-start(f32[1024]{0:T(1024)} %param.16) | copy-start | bytes 12292
  80.1 0.8 copy-start.15
  83.0 89.7 %all-gather.9.cloned.1.call-start = ((), (), s32[]{:S(2)}) async-start(), calls=%async_computation.8 | async-start | bytes 2621440 | tf_op jit(solution)/shard_map/all_gather | solution.py:111
  83.8 135.7 %all-gather.7.cloned.1.call-start = ((), (), s32[]{:S(2)}) async-start(), calls=%async_computation.6 | async-start | bytes 2621440 | tf_op jit(solution)/shard_map/all_gather | solution.py:100
  129.2 146.4 %reduce-scatter.9.cloned.1.call-start = ((), (), s32[]{:S(2)}) async-start(), calls=%async_computation.9 | async-start | bytes 2621440 | tf_op jit(solution)/shard_map/reduce_scatter | solution.py:45
  227.7 1.3 copy-start.27
  232.8 92.4 %all-gather.11.cloned.1.call-start = ((), (), s32[]{:S(2)}) async-start(), calls=%async_computation.10 | async-start | bytes 2621440 | tf_op jit(solution)/shard_map/all_gather | solution.py:123
  279.8 198.1 %all-reduce.4.cloned.1.call-start = ((), (), s32[]{:S(2)}) async-start(), calls=%async_computation.12 | async-start | bytes 12582912 | tf_op jit(solution)/shard_map/psum | solution.py:52
  280.3 6.1 %copy-start.25 = (bf16[1024,1024]{1,0:T(8,128)(2,1)S(1)}, bf16[1024,1024]{1,0:T(8,128)(2,1)}, u32[]{:S(2)}) copy-start(bf16[1024,1024]{1,0:T(8,128)(2,1)} %all-gather.9.cloned.1.call-done) | copy-start | bytes 6291460
  280.3 6.1 %copy-start.26 = (f32[1024,1024]{1,0:T(8,128)S(1)}, f32[1024,1024]{1,0:T(8,128)}, u32[]{:S(2)}) copy-start(f32[1024,1024]{1,0:T(8,128)} %get-tuple-element.51) | copy-start | bytes 12582916
  286.4 38.8 %copy-start.20 = (bf16[256,1024]{1,0:T(8,128)(2,1)S(1)}, bf16[256,1024]{1,0:T(8,128)(2,1)}, u32[]{:S(2)}) copy-start(bf16[256,1024]{1,0:T(8,128)(2,1)} %param.12) | copy-start | bytes 1572868
  290.5 37.3 %copy-start.10 = (pred[512,1024]{1,0:T(8,128)(4,1)S(1)}, pred[512,1024]{1,0:T(8,128)(4,1)}, u32[]{:S(2)}) copy-start(pred[512,1024]{1,0:T(8,128)(4,1)} %get-tuple-element.43) | copy-start | bytes 1572868
  325.2 7.7 %slice-start.2 = ((s8[8388608]{0:T(1024)(128)(4,1)}), s8[4194304]{0:T(1024)(128)(4,1)S(1)}, s32[]{:S(2)}) async-start(s8[8388608]{0:T(1024)(128)(4,1)} %bitcast.84), calls=%async_computation.15 | async-start | bytes 8388608
  327.8 5.2 slice-start.3
  327.8 5.2 copy-start.22
  327.8 10.9 %slice-start = ((s8[8388608]{0:T(1024)(128)(4,1)}), s8[4194304]{0:T(1024)(128)(4,1)S(1)}, s32[]{:S(2)}) async-start(s8[8388608]{0:T(1024)(128)(4,1)} %bitcast.82), calls=%async_computation.13 | async-start | bytes 8388608
  333.0 5.7 slice-start.1
  333.0 5.7 copy-start.8
  354.9 2.1 copy-start.12
  361.4 3.7 copy-start.4
  365.1 1.2 copy-start.17
  365.1 1.4 copy-start.16
  366.1 3.6 copy-start.18
  374.3 150.0 %reduce-scatter.11.cloned.1.call-start = ((), (), s32[]{:S(2)}) async-start(), calls=%async_computation.11 | async-start | bytes 2621440 | tf_op jit(solution)/shard_map/reduce_scatter | solution.py:45
  379.0 191.9 %reduce-scatter.7.cloned.1.call-start = ((), (), s32[]{:S(2)}) async-start(), calls=%async_computation.7 | async-start | bytes 2621440 | tf_op jit(solution)/shard_map/reduce_scatter | solution.py:103
  477.9 5.5 copy-start.14
  483.5 2.5 copy-start.13
  486.0 38.4 %copy-start.24 = (f32[1024]{0:T(1024)S(1)}, f32[1024]{0:T(1024)}, u32[]{:S(2)}) copy-start(f32[1024]{0:T(1024)} %param.15) | copy-start | bytes 12292
  486.0 84.9 %copy-start.6 = (bf16[256,1024]{1,0:T(8,128)(2,1)S(1)}, bf16[256,1024]{1,0:T(8,128)(2,1)}, u32[]{:S(2)}) copy-start(bf16[256,1024]{1,0:T(8,128)(2,1)} %reduce-scatter.5.cloned.1.call-done) | copy-start | bytes 1572868
  486.0 88.3 %copy-start.1 = (bf16[1024,1024]{1,0:T(8,128)(2,1)S(1)}, bf16[1024,1024]{1,0:T(8,128)(2,1)}, u32[]{:S(2)}) copy-start(bf16[1024,1024]{1,0:T(8,128)(2,1)} %param.13) | copy-start | bytes 6291460
Sparse Core Ops, SparseCore 0:
  10.8 48.6 all-gather.4
  83.2 42.5 reduce-scatter.4
  127.4 45.2 all-gather.8
  174.8 44.6 all-gather.6
  232.9 42.5 reduce-scatter.8
  280.0 45.2 all-gather.10
  374.4 103.4 all-reduce.3
  480.3 43.9 reduce-scatter.10
  526.6 44.2 reduce-scatter.6

commit v2 on v1

v2 whole, which is shorter than its diff:
```python
import functools
import math

import jax
import jax.numpy as jnp
from jax import lax
from jax.experimental import pallas as pl
from jax.experimental.pallas import tpu as pltpu
from jax.sharding import Mesh
from jax.sharding import PartitionSpec as P

HEAD = 64
EPSILON = 1e-06
NEGATIVE = -1e30
MEMBERS = 4
LOG2E = math.log2(math.e)
GELU_A = math.sqrt(2.0 / math.pi)
GELU_B = 0.044715
AXES = ("col", "core", "pair", "zz")
BF16 = jnp.bfloat16
F32 = jnp.float32
VMEM_LIMIT = 60 << 20
MESH_ID = pl.DeviceIdType.MESH


def dot_nn(a, b):
    return lax.dot_general(a, b, (((1,), (0,)), ((), ())), preferred_element_type=F32)


def dot_nt(a, b):
    return lax.dot_general(a, b, (((1,), (1,)), ((), ())), preferred_element_type=F32)


def dot_tn(a, b):
    return lax.dot_general(a, b, (((0,), (0,)), ((), ())), preferred_element_type=F32)


def flip(bit, amount):
    return bit + amount - 2 * bit * amount


class Place:
    def __init__(self):
        self.col = lax.axis_index("col")
        self.core = lax.axis_index("core")
        self.pair = lax.axis_index("pair")
        self.zz = lax.axis_index("zz")
        self.swapped = self.core != self.pair
        self.stays = self.core == self.pair
        self.me = self.member(0, 0)

    def member(self, other_core, other_chip):
        return 2 * flip(self.core, other_core) + flip(self.zz, other_chip)

    def sibling(self):
        return {"core": 1 - self.core}

    def across(self):
        return {"zz": 1 - self.zz}

    def trade(self):
        return {"pair": 1 - self.pair, "core": 1 - self.core}

    def column(self, bit):
        step = 1 << bit
        here = lax.rem(lax.div(self.col, step), 2)
        return {"col": self.col + step * (1 - 2 * here)}


class Wire:
    def __init__(self, send_sems, recv_sems):
        self.send_sems = send_sems
        self.recv_sems = recv_sems
        self.used = 0

    def copy(self, src, dst, target, got=None):
        number = self.used
        self.used += 1
        return Transfer(
            src, dst, target, dst if got is None else got,
            self.send_sems.at[number], self.recv_sems.at[number],
        )


class Transfer:
    def __init__(self, src, dst, target, got, send_sem, recv_sem):
        self.args = (src, dst, target, got, send_sem, recv_sem)

    def start(self):
        src, dst, target, _, send_sem, recv_sem = self.args
        pltpu.make_async_remote_copy(
            src_ref=src, dst_ref=dst, send_sem=send_sem, recv_sem=recv_sem,
            device_id=target, device_id_type=MESH_ID,
        ).start()

    def wait_send(self):
        src, dst, target, _, send_sem, recv_sem = self.args
        pltpu.make_async_remote_copy(
            src_ref=src, dst_ref=dst, send_sem=send_sem, recv_sem=recv_sem,
            device_id=target, device_id_type=MESH_ID,
        ).wait_send()

    def wait_recv(self):
        _, _, target, got, send_sem, recv_sem = self.args
        pltpu.make_async_remote_copy(
            src_ref=got, dst_ref=got, send_sem=send_sem, recv_sem=recv_sem,
            device_id=target, device_id_type=MESH_ID,
        ).wait_recv()


def meet(targets):
    barrier = pltpu.get_barrier_semaphore()
    for target in targets:
        pl.semaphore_signal(barrier, inc=1, device_id=target, device_id_type=MESH_ID)
    pl.semaphore_wait(barrier, len(targets))


class Gather:
    def __init__(self, wire, place, whole):
        me, near = place.me, place.member(1, 0)
        far, corner = place.member(0, 1), place.member(1, 1)
        self.to_near = wire.copy(whole.at[me], whole.at[me], place.sibling(), whole.at[near])
        self.to_far = wire.copy(whole.at[me], whole.at[me], place.across(), whole.at[far])
        self.relay = wire.copy(whole.at[far], whole.at[far], place.sibling(), whole.at[corner])

    def start(self):
        self.to_far.start()
        self.to_near.start()

    def take_near(self):
        self.to_near.wait_recv()

    def take_far(self):
        self.to_far.wait_recv()
        self.relay.start()

    def take_corner(self):
        self.relay.wait_recv()

    def drain(self):
        self.to_near.wait_send()
        self.to_far.wait_send()
        self.relay.wait_send()


class Scatter:
    def __init__(self, wire, place, part, near_in, joined, far_in):
        self.place, self.part = place, part
        self.near_in, self.joined, self.far_in = near_in, joined, far_in
        corner, near = place.member(1, 1), place.member(1, 0)
        self.corner = wire.copy(part.at[corner], near_in.at[0], place.sibling())
        self.near = wire.copy(part.at[near], near_in.at[1], place.sibling())
        self.far = wire.copy(joined, far_in, place.across())

    def send_corner(self):
        self.corner.start()

    def send_near(self):
        self.near.start()

    def send_far(self):
        self.corner.wait_recv()
        far = self.place.member(0, 1)

        def rows(step, carry):
            at = pl.ds(pl.multiple_of(step * 64, 64), 64)
            total = self.part[far, at].astype(F32) + self.near_in[0, at].astype(F32)
            self.joined[at] = total.astype(BF16)
            return carry

        lax.fori_loop(0, self.joined.shape[0] // 64, rows, 0)
        self.far.start()

    def wait(self):
        self.near.wait_recv()
        self.far.wait_recv()

    def total(self, at):
        return (
            self.part[self.place.me, at].astype(F32)
            + self.near_in[1, at].astype(F32)
            + self.far_in[at].astype(F32)
        )

    def drain(self):
        self.corner.wait_send()
        self.near.wait_send()
        self.far.wait_send()


def each_rows(count, size, body):
    def step(number, carry):
        body(pl.ds(pl.multiple_of(number * size, size), size))
        return carry

    lax.fori_loop(0, count // size, step, 0)


def scatter_shapes(rows, width):
    return [
        pltpu.VMEM((MEMBERS, rows, width), BF16),
        pltpu.VMEM((2, rows, width), BF16),
        pltpu.VMEM((rows, width), BF16),
        pltpu.VMEM((rows, width), BF16),
    ]


def visible_tile(first_ref, block, tile, rows):
    key_at = tile * rows + lax.broadcasted_iota(jnp.int32, (rows, rows), 0)
    query_at = block * rows + lax.broadcasted_iota(jnp.int32, (rows, rows), 1)
    first = first_ref[0:1, pl.ds(pl.multiple_of(block * rows, rows), rows)]
    return (key_at >= first) & (key_at <= query_at)


def swap_order(step):
    return lax.rem(step, 2), lax.div(step, 2)


def forward_kernel(
    items,
    x_own, dy_own, lengths, gain_attn, gain_mlp, wq, wa, wi, wo,
    heads_out, keys_t, att_t, lse, first, normed, grads, outs, resid, grad_resid, gain_part,
    wq_m, wa_m, x_keep,
    wi_m, wo_m, x_all, dy_all, values_t, first_near, scores, acc_t, normed_mlp, active, grad_hidden,
    part1, near1, joined1, far1, part3, near3, joined3, far3,
    send_sems, recv_sems, local_sems,
):
    place = Place()
    wire = Wire(send_sems, recv_sems)
    rows, width = x_own.shape
    heads = heads_out.shape[1]
    me = place.me
    frame_count = MEMBERS * rows
    hidden_units = wi.shape[1]

    near = place.member(1, 0)
    x_trade = wire.copy(x_own, x_all.at[near], place.trade(), x_all.at[me])
    dy_trade = wire.copy(dy_own, dy_all.at[near], place.trade(), dy_all.at[me])
    first_trade = wire.copy(first_near.at[0], first_near.at[1], place.sibling())

    quarter = lax.rem(place.col, MEMBERS)
    weights = []
    for source, target, axis in ((wq, wq_m, 1), (wa, wa_m, 0), (wi, wi_m, 0), (wo, wo_m, 0)):
        depth = source.shape[axis] // MEMBERS

        def cut(ref, start, size, axis=axis):
            window = pl.ds(pl.multiple_of(start, size), size)
            return ref.at[:, window] if axis == 1 else ref.at[window]

        other = quarter + 1 - 2 * lax.rem(quarter, 2)
        duo = lax.div(quarter, 2)
        mine = cut(target, quarter * depth, depth)
        steps = (
            wire.copy(cut(source, quarter * depth, depth), mine, place.trade()),
            wire.copy(mine, mine, place.column(0), cut(target, other * depth, depth)),
            wire.copy(
                cut(target, duo * 2 * depth, 2 * depth),
                cut(target, duo * 2 * depth, 2 * depth),
                place.column(1),
                cut(target, (1 - duo) * 2 * depth, 2 * depth),
            ),
        )
        local = pltpu.make_async_copy(source, target, local_sems.at[len(weights)])
        weights.append((steps, local))

    def when_swapped(action):
        pl.when(place.swapped)(action)

    def when_stays(action):
        pl.when(place.stays)(action)

    meet([place.sibling(), place.across(), place.trade(), place.column(0), place.column(1)])

    @when_swapped
    def _():
        x_trade.start()
        weights[0][0][0].start()

    @when_stays
    def _():
        x_all[me] = x_own[...]
        dy_all[me] = dy_own[...]
        for _, local in weights:
            local.start()

    position = lax.broadcasted_iota(jnp.int32, (8, frame_count), 1)
    begin = jnp.zeros((8, frame_count), jnp.int32)
    end = jnp.int32(0)
    for item in range(items):
        size = lengths[0, item]
        end = end + size
        begin = begin + jnp.where(position >= end, size, 0)
    first_near[0] = jnp.where(position >= end, position, begin)
    first_trade.start()

    @when_swapped
    def _():
        x_trade.wait_recv()

    gather_x = Gather(wire, place, x_all)
    gather_x.start()
    gain = gain_attn[...]

    def norm_block(member):
        def some(at):
            values = x_all[member, at].astype(F32)
            scale = lax.rsqrt(jnp.mean(values * values, axis=-1, keepdims=True) + EPSILON)
            normed[member, at] = (values * scale * gain).astype(BF16)

        each_rows(rows, 64, some)

    norm_block(me)
    x_keep[...] = x_all[me]
    first_trade.wait_recv()

    @when_swapped
    def _():
        first[...] = first_near[1]
        weights[0][0][0].wait_recv()
        weights[0][0][1].start()
        dy_trade.start()
        for steps, _ in weights[1:]:
            steps[0].start()

    @when_stays
    def _():
        first[...] = first_near[0]

    gather_x.take_near()
    norm_block(place.member(1, 0))

    @when_swapped
    def _():
        weights[0][0][1].wait_recv()
        weights[0][0][2].start()

    gather_x.take_far()
    norm_block(place.member(0, 1))
    gather_x.take_corner()
    norm_block(place.member(1, 1))

    @when_swapped
    def _():
        weights[0][0][2].wait_recv()

    @when_stays
    def _():
        weights[0][1].wait()

    def project(member, carry):
        source = normed[member]
        for kind in range(3):
            block = dot_nn(source, wq_m[kind])
            narrow = block.astype(BF16)
            for head in range(heads):
                heads_out[kind, head, member] = narrow[:, head * HEAD : (head + 1) * HEAD]
            if kind == 1:
                keys_t[member] = block.T.astype(BF16)
            if kind == 2:
                values_t[member] = block.T.astype(BF16)
        return carry

    lax.fori_loop(0, MEMBERS, project, 0)

    @when_swapped
    def _():
        dy_trade.wait_recv()

    gather_dy = Gather(wire, place, dy_all)
    gather_dy.start()

    @when_swapped
    def _():
        for steps, _ in weights[1:]:
            steps[0].wait_recv()
            steps[1].start()
        weights[1][0][1].wait_recv()
        weights[1][0][2].start()
        weights[1][0][2].wait_recv()

    @when_stays
    def _():
        weights[1][1].wait()

    shift = (HEAD ** -0.5) * LOG2E
    scatter1 = Scatter(wire, place, part1, near1, joined1, far1)

    def attend(step, carry):
        flip_core, flip_chip = swap_order(3 - step)
        block = place.member(flip_core, flip_chip)

        def score(tile, peaks):
            seen = visible_tile(first, block, tile, rows)
            higher = []
            for head in range(heads):
                raw = dot_nt(heads_out[1, head, tile], heads_out[0, head, block])
                raw = jnp.where(seen, raw, NEGATIVE)
                scores[head, tile] = raw
                higher.append(jnp.maximum(peaks[head], jnp.max(raw, axis=0, keepdims=True)))
            return tuple(higher)

        low = jnp.full((1, rows), NEGATIVE, F32)
        peaks = lax.fori_loop(0, block + 1, score, (low,) * heads)
        acc_t[...] = jnp.zeros_like(acc_t)

        def weigh(tile, totals):
            sums = []
            for head in range(heads):
                weight = jnp.exp2((scores[head, tile] - peaks[head]) * shift)
                sums.append(totals[head] + jnp.sum(weight, axis=0, keepdims=True))
                at = slice(head * HEAD, (head + 1) * HEAD)
                acc_t[at] += dot_nn(values_t[tile, at], weight.astype(BF16))
            return tuple(sums)

        none = jnp.zeros((1, rows), F32)
        totals = lax.fori_loop(0, block + 1, weigh, (none,) * heads)
        for head in range(heads):
            at = slice(head * HEAD, (head + 1) * HEAD)
            acc_t[at] = acc_t[at] / totals[head]
            lse[block, head : head + 1] = peaks[head] * shift + jnp.log2(totals[head])
        att_t[block] = acc_t[...].astype(BF16)
        attended = acc_t[...].T.astype(BF16)
        part1[block] = dot_nn(attended, wa_m[...]).astype(BF16)

        @pl.when(step == 0)
        def _():
            scatter1.send_corner()

        @pl.when(step == 1)
        def _():
            scatter1.send_far()

        @pl.when(step == 2)
        def _():
            scatter1.send_near()

        return carry

    lax.fori_loop(0, MEMBERS, attend, 0)

    gather_dy.take_near()
    gather_dy.take_far()
    gather_dy.take_corner()

    @when_swapped
    def _():
        for steps, _ in weights[2:]:
            steps[1].wait_recv()
            steps[2].start()

    scatter1.wait()
    gain2 = gain_mlp[...]

    def add_resid(at):
        total = x_all[me, at].astype(F32) + scatter1.total(at)
        resid[at] = total
        scale = lax.rsqrt(jnp.mean(total * total, axis=-1, keepdims=True) + EPSILON)
        normed_mlp[me, at] = (total * scale * gain2).astype(BF16)

    each_rows(rows, 64, add_resid)
    gather_n = Gather(wire, place, normed_mlp)
    gather_n.start()

    @when_swapped
    def _():
        for steps, _ in weights[2:]:
            steps[2].wait_recv()

    @when_stays
    def _():
        for _, local in weights[2:]:
            local.wait()

    span = 256
    scatter3 = Scatter(wire, place, part3, near3, joined3, far3)

    def feed(step, carry):
        flip_core = jnp.where((step == 1) | (step == 2), 1, 0)
        flip_chip = jnp.where(step >= 2, 1, 0)
        block = place.member(flip_core, flip_chip)

        @pl.when(step == 1)
        def _():
            gather_n.take_near()

        @pl.when(step == 2)
        def _():
            gather_n.take_far()
            gather_n.take_corner()

        def units(number, inner):
            at = pl.ds(pl.multiple_of(number * span, span), span)
            hidden = dot_nn(normed_mlp[block], wi_m[:, at])
            grad_active = dot_nt(dy_all[block], wo_m[at])
            square = hidden * hidden
            bend = jnp.tanh(GELU_A * hidden * (1.0 + GELU_B * square))
            half = 0.5 * (1.0 + bend)
            active[block, :, at] = (hidden * half).astype(BF16)
            slope = half + 0.5 * hidden * (1.0 - bend * bend) * (
                GELU_A * (1.0 + 3.0 * GELU_B * square)
            )
            grad_hidden[block, :, at] = (grad_active * slope).astype(BF16)
            return inner

        lax.fori_loop(0, hidden_units // span, units, 0)

        def features(number, inner):
            at = pl.ds(pl.multiple_of(number * span, span), span)
            part3[block, :, at] = dot_nt(grad_hidden[block], wi_m[at]).astype(BF16)
            outs[block, :, at] = dot_nn(active[block], wo_m[:, at]).astype(BF16)
            return inner

        lax.fori_loop(0, width // span, features, 0)

        @pl.when(step == 1)
        def _():
            scatter3.send_near()

        @pl.when(step == 2)
        def _():
            scatter3.send_corner()

        @pl.when(step == 3)
        def _():
            scatter3.send_far()

        return carry

    lax.fori_loop(0, MEMBERS, feed, 0)

    def weight_grads(number, carry):
        at = pl.ds(pl.multiple_of(number * span, span), span)
        down = pl.ds(pl.multiple_of(width + number * span, span), span)
        left = normed_mlp[:, :, at].reshape(frame_count, span)
        grads[at] = dot_tn(left, grad_hidden[...].reshape(frame_count, hidden_units)).astype(BF16)
        left = active[:, :, at].reshape(frame_count, span)
        grads[down] = dot_tn(left, dy_all[...].reshape(frame_count, width)).astype(BF16)
        return carry

    lax.fori_loop(0, width // span, weight_grads, 0)

    scatter3.wait()
    gain_part[...] = jnp.zeros_like(gain_part)

    def norm_back(at):
        grad = scatter3.total(at)
        values = resid[at]
        scale = lax.rsqrt(jnp.mean(values * values, axis=-1, keepdims=True) + EPSILON)
        gain_part[0:1] += jnp.sum(grad * values * scale, axis=0, keepdims=True)
        scaled = grad * gain2
        mean = jnp.mean(scaled * values, axis=-1, keepdims=True)
        grad_resid[at] = (
            dy_all[me, at].astype(F32) + scale * scaled - values * (scale * scale * scale) * mean
        )

    each_rows(rows, 64, norm_back)

    for one in (gather_x, gather_dy, gather_n, scatter1, scatter3):
        one.drain()
    first_trade.wait_send()

    @when_swapped
    def _():
        x_trade.wait_send()
        dy_trade.wait_send()
        for steps, _ in weights:
            for step in steps:
                step.wait_send()


def vmem(shape, kind):
    return pltpu.VMEM(shape, kind)


def forward_call(x_own, dy_own, lengths, gain_attn, gain_mlp, wq, wa, wi, wo):
    rows, width = x_own.shape
    heads = wa.shape[0] // HEAD
    features = wa.shape[0]
    units = wi.shape[1]
    frames = MEMBERS * rows
    outputs = [
        ((3, heads, MEMBERS, rows, HEAD), BF16),
        ((MEMBERS, features, rows), BF16),
        ((MEMBERS, features, rows), BF16),
        ((MEMBERS, 8, rows), F32),
        ((8, frames), jnp.int32),
        ((MEMBERS, rows, width), BF16),
        ((width + units, width), BF16),
        ((MEMBERS, rows, width), BF16),
        ((rows, width), F32),
        ((rows, width), F32),
        ((8, width), F32),
        (wq.shape, BF16),
        (wa.shape, BF16),
        ((rows, width), BF16),
    ]
    block = pl.BlockSpec(memory_space=pltpu.VMEM)
    whole = pl.BlockSpec(memory_space=pl.ANY)
    members = (MEMBERS, rows, width)
    return pl.pallas_call(
        functools.partial(forward_kernel, lengths.shape[1]),
        out_shape=[jax.ShapeDtypeStruct(shape, kind) for shape, kind in outputs],
        in_specs=[block, block, pl.BlockSpec(memory_space=pltpu.SMEM), block, block]
        + [whole] * 4,
        out_specs=[block] * len(outputs),
        scratch_shapes=[
            vmem(wi.shape, BF16),
            vmem(wo.shape, BF16),
            vmem(members, BF16),
            vmem(members, BF16),
            vmem((MEMBERS, features, rows), BF16),
            vmem((2, 8, frames), jnp.int32),
            vmem((heads, MEMBERS, rows, rows), F32),
            vmem((features, rows), F32),
            vmem(members, BF16),
            vmem((MEMBERS, rows, units), BF16),
            vmem((MEMBERS, rows, units), BF16),
        ]
        + scatter_shapes(rows, width) * 2
        + [
            pltpu.SemaphoreType.DMA((32,)),
            pltpu.SemaphoreType.DMA((32,)),
            pltpu.SemaphoreType.DMA((4,)),
        ],
        compiler_params=pltpu.CompilerParams(
            collective_id=0, has_side_effects=True, vmem_limit_bytes=VMEM_LIMIT
        ),
        name="forward",
    )(x_own, dy_own, lengths, gain_attn, gain_mlp, wq, wa, wi, wo)


def backward_kernel(
    bits,
    heads_in, keys_t, att_t, lse, first, normed, outs, resid, grad_resid, gain_in, wq, wa, x_keep,
    gain_attn,
    output, grad_frames, grads_attn, gains_out,
    grad_all, top_t, grad_qt, grad_k, grad_v, projected, gain_sum, gain_got, moved, moved_in,
    out_keep, out_in,
    near2, joined2, far2, part4, near4, joined4, far4,
    send_sems, recv_sems,
):
    place = Place()
    wire = Wire(send_sems, recv_sems)
    rows, width = x_keep.shape
    heads = heads_in.shape[1]
    features = heads * HEAD
    me = place.me
    frame_count = MEMBERS * rows

    meet(
        [place.sibling(), place.across(), place.trade()]
        + [{"pair": 1 - place.pair}]
        + [place.column(bit) for bit in range(bits)]
    )

    grad_all[me] = grad_resid[...].astype(BF16)
    gather_g = Gather(wire, place, grad_all)
    gather_g.start()
    scatter2 = Scatter(wire, place, outs, near2, joined2, far2)
    scatter2.send_corner()
    scatter2.send_near()
    grad_k[...] = jnp.zeros_like(grad_k)
    grad_v[...] = jnp.zeros_like(grad_v)
    shift = (HEAD ** -0.5) * LOG2E
    scaling = HEAD ** -0.5

    def block_back(step, carry):
        flip_core, flip_chip = swap_order(step)
        block = place.member(flip_core, flip_chip)

        @pl.when(step == 1)
        def _():
            gather_g.take_near()
            scatter2.send_far()

        @pl.when(step == 2)
        def _():
            gather_g.take_far()

        @pl.when(step == 3)
        def _():
            gather_g.take_corner()

        source = grad_all[block]
        top = dot_nt(source, wa[...]).astype(BF16)
        turned = dot_nt(wa[...], source).astype(BF16)
        top_t[...] = turned
        tops = [top[:, head * HEAD : (head + 1) * HEAD] for head in range(heads)]
        product = turned.astype(F32) * att_t[block].astype(F32)
        deltas = [
            jnp.sum(product[head * HEAD : (head + 1) * HEAD], axis=0, keepdims=True)
            for head in range(heads)
        ]
        grad_qt[...] = jnp.zeros_like(grad_qt)

        def tiles(tile, inner):
            seen = visible_tile(first, block, tile, rows)
            for head in range(heads):
                at = slice(head * HEAD, (head + 1) * HEAD)
                query = heads_in[0, head, block]
                raw = dot_nt(heads_in[1, head, tile], query)
                prob = jnp.where(
                    seen, jnp.exp2(raw * shift - lse[block, head : head + 1]), 0.0
                )
                grad_prob = dot_nt(heads_in[2, head, tile], tops[head])
                grad_score = (prob * (grad_prob - deltas[head])).astype(BF16)
                grad_v[head, tile] += dot_nn(prob.astype(BF16), tops[head])
                grad_k[head, tile] += dot_nn(grad_score, query)
                grad_qt[at] += dot_nn(keys_t[tile, at], grad_score)
            return inner

        lax.fori_loop(0, block + 1, tiles, 0)
        projected[0, block] = (grad_qt[...].T * scaling).astype(BF16)
        return carry

    lax.fori_loop(0, MEMBERS, block_back, 0)

    scatter4 = Scatter(wire, place, part4, near4, joined4, far4)

    def inputs_back(step, carry):
        flip_core, flip_chip = swap_order(3 - step)
        block = place.member(flip_core, flip_chip)
        for head in range(heads):
            at = slice(head * HEAD, (head + 1) * HEAD)
            projected[1, block, :, at] = (grad_k[head, block] * scaling).astype(BF16)
            projected[2, block, :, at] = grad_v[head, block].astype(BF16)
        span = 256

        def columns(number, inner):
            down = pl.ds(pl.multiple_of(number * span, span), span)
            total = dot_nt(projected[0, block], wq[0, down])
            total += dot_nt(projected[1, block], wq[1, down])
            total += dot_nt(projected[2, block], wq[2, down])
            part4[block, :, down] = total.astype(BF16)
            return inner

        lax.fori_loop(0, width // span, columns, 0)

        @pl.when(step == 0)
        def _():
            scatter4.send_corner()

        @pl.when(step == 1)
        def _():
            scatter4.send_far()

        @pl.when(step == 2)
        def _():
            scatter4.send_near()

        return carry

    lax.fori_loop(0, MEMBERS, inputs_back, 0)

    for kind in range(3):
        right = projected[kind].reshape(frame_count, features)

        def weight_grads(number, carry, kind=kind, right=right):
            at = pl.ds(pl.multiple_of(number * 256, 256), 256)
            to = pl.ds(pl.multiple_of(kind * width + number * 256, 256), 256)
            left = normed[:, :, at].reshape(frame_count, 256)
            grads_attn[to] = dot_tn(left, right).astype(BF16)
            return carry

        lax.fori_loop(0, width // 256, weight_grads, 0)

    def out_grads(number, carry):
        at = pl.ds(pl.multiple_of(number * features, features), features)
        to = pl.ds(pl.multiple_of(3 * width + number * features, features), features)
        total = dot_nn(att_t[0], grad_all[0, :, at])
        for member in range(1, MEMBERS):
            total += dot_nn(att_t[member], grad_all[member, :, at])
        grads_attn[to] = total.astype(BF16)
        return carry

    lax.fori_loop(0, width // features, out_grads, 0)

    scatter2.wait()

    def finish_output(at):
        out_keep[at] = (resid[at] + scatter2.total(at)).astype(BF16)

    each_rows(rows, 64, finish_output)
    out_trade = wire.copy(out_keep, out_in, place.trade())

    @pl.when(place.swapped)
    def _():
        out_trade.start()

    scatter4.wait()
    gain = gain_attn[...]
    gain_sum[...] = jnp.zeros_like(gain_sum)
    gain_sum[0:1] = gain_in[0:1]

    def finish_frames(at):
        grad = scatter4.total(at)
        values = x_keep[at].astype(F32)
        scale = lax.rsqrt(jnp.mean(values * values, axis=-1, keepdims=True) + EPSILON)
        gain_sum[1:2] += jnp.sum(grad * values * scale, axis=0, keepdims=True)
        scaled = grad * gain
        mean = jnp.mean(scaled * values, axis=-1, keepdims=True)
        total = grad_resid[at] + scale * scaled - values * (scale * scale * scale) * mean
        grad_frames[at] = total
        moved[at] = total.astype(BF16)

    each_rows(rows, 64, finish_frames)
    frames_trade = wire.copy(moved, moved_in, place.trade())

    @pl.when(place.swapped)
    def _():
        frames_trade.start()

    partners = [place.sibling(), place.across(), {"pair": 1 - place.pair}]
    partners += [place.column(bit) for bit in range(bits)]
    for number, partner in enumerate(partners):
        trade = wire.copy(gain_sum.at[pl.ds(8 * number, 8)], gain_got.at[number], partner)
        trade.start()
        trade.wait_recv()
        here = slice(8 * number, 8 * number + 8)
        gain_sum[8 * number + 8 : 8 * number + 16] = gain_sum[here] + gain_got[number]
        trade.wait_send()
    gains_out[...] = gain_sum[8 * len(partners) : 8 * len(partners) + 8]

    @pl.when(place.swapped)
    def _():
        out_trade.wait_recv()
        output[...] = out_in[...]
        frames_trade.wait_recv()
        grad_frames[...] = moved_in[...].astype(F32)
        out_trade.wait_send()
        frames_trade.wait_send()

    @pl.when(place.stays)
    def _():
        output[...] = out_keep[...]

    for one in (gather_g, scatter2, scatter4):
        one.drain()


def backward_call(bits, saved, gain_attn):
    (heads_in, keys_t, att_t, lse, first, normed, _, outs, resid, grad_resid, gain_part,
     wq, wa, x_keep) = saved
    rows, width = x_keep.shape
    features = wa.shape[0]
    heads = features // HEAD
    members = (MEMBERS, rows, width)
    steps = 3 + bits
    block = pl.BlockSpec(memory_space=pltpu.VMEM)
    outputs = [
        ((rows, width), BF16),
        ((rows, width), F32),
        ((4 * width, features), BF16),
        ((8, width), F32),
    ]
    args = (heads_in, keys_t, att_t, lse, first, normed, outs, resid, grad_resid, gain_part,
            wq, wa, x_keep, gain_attn)
    return pl.pallas_call(
        functools.partial(backward_kernel, bits),
        out_shape=[jax.ShapeDtypeStruct(shape, kind) for shape, kind in outputs],
        in_specs=[block] * len(args),
        out_specs=[block] * len(outputs),
        scratch_shapes=[
            vmem(members, BF16),
            vmem((features, rows), BF16),
            vmem((features, rows), F32),
            vmem((heads, MEMBERS, rows, HEAD), F32),
            vmem((heads, MEMBERS, rows, HEAD), F32),
            vmem((3, MEMBERS, rows, features), BF16),
            vmem((8 * steps + 8, width), F32),
            vmem((steps, 8, width), F32),
            vmem((rows, width), BF16),
            vmem((rows, width), BF16),
            vmem((rows, width), BF16),
            vmem((rows, width), BF16),
        ]
        + scatter_shapes(rows, width)[1:]
        + scatter_shapes(rows, width)
        + [pltpu.SemaphoreType.DMA((24,)), pltpu.SemaphoreType.DMA((24,))],
        compiler_params=pltpu.CompilerParams(
            collective_id=1, has_side_effects=True, vmem_limit_bytes=VMEM_LIMIT
        ),
        name="backward",
    )(*args)


def spread_grads(grads):
    piece = lax.psum_scatter(grads, ("col", "pair"), scatter_dimension=0, tiled=True)
    moves = []
    for core in range(2):
        for pair in range(2):
            source = core * 2 + pair
            moves.append((source, source if core == pair else 3 - source))
    piece = lax.ppermute(piece, ("core", "pair"), moves)
    return lax.all_gather(piece, ("col", "core"), axis=0, tiled=True)


def per_device(bits, frames, lengths, wq, wa, wi, wo, gain_attn, gain_mlp, cotangent):
    width = frames.shape[1]
    features = wa.shape[0]
    first_gain = gain_attn.reshape(1, width)
    second_gain = gain_mlp.reshape(1, width)
    saved = forward_call(frames, cotangent, lengths, first_gain, second_gain, wq, wa, wi, wo)
    grads_mlp = spread_grads(saved[6]).astype(F32)
    output, grad_frames, grads_attn, gains = backward_call(bits, saved, first_gain)
    grads_attn = spread_grads(grads_attn).astype(F32)
    grad_wq = grads_attn[: 3 * width].reshape(3, width, features)
    turned = grads_attn[3 * width :].reshape(width // features, features, features)
    grad_wa = jnp.transpose(turned, (1, 0, 2)).reshape(features, width)
    return (
        output,
        grad_frames,
        grad_wq,
        grad_wa,
        grads_mlp[:width],
        grads_mlp[width:],
        gains[1],
        gains[0],
    )


def solution(mesh):
    batches = mesh.shape["dp"]
    bits = (batches // 2).bit_length() - 1
    inner = Mesh(mesh.devices.reshape(batches // 2, 2, 2, 2), AXES)
    dp, mp = ("col", "core"), ("pair", "zz")
    rows = P(dp + mp, None)
    weights = (P(None, None, mp), P(mp, None), P(None, mp), P(mp, None))
    return jax.shard_map(
        functools.partial(per_device, bits),
        mesh=inner,
        in_specs=(rows, P(dp, None)) + weights + (P(), P(), rows),
        out_specs=(rows, rows) + weights + (P(), P()),
        check_vma=False,
    )
```

time: 590 us -> 564 us (0.956); the launches traced: 581 us -> 564 us
  Pallas kernels: 0 us -> 217 us
  matrix products: 93.5 us -> 0 us
  waiting for transfers between devices: 378 us -> 313 us
  other arithmetic: 42.8 us -> 0 us
  blocking collectives: 42.6 us -> 0 us
  local copies, waits for them, and re-layouts: 8.28 us -> 15.6 us
    pallas_call x0 -> x2, Pallas kernels: none -> 217 us  [the longest x1 137 us: forward_call(): pl.pallas_call(functools.partial(forward_kernel, lengths.shape[1]), out_s...]
    reduce_scatter x4 -> x2, waiting for transfers between devices: 123 us -> 252 us  [spread_grads(): lax.psum_scatter(grads, ('col', 'pair'), scatter_dimension=0, tiled=True)]
    all_gather x4 -> x2, waiting for transfers between devices: 163 us -> 60.6 us  [spread_grads(): return lax.all_gather(piece, ('col', 'core'), axis=0, tiled=True)]
    dot_general x24 -> x0, matrix products: 93.5 us -> none  [the longest x2 11.5 us: per_device(): jnp.einsum('bhd,khd->hbk', grad_rows, values_all, preferred_element_type=...]
    psum x1 -> x0, waiting for transfers between devices: 91.6 us -> none  [batch_sum(): return tuple((total.astype(jnp.float32) for total in lax.psum(sent, 'dp')))]
    psum x1 -> x0, blocking collectives: 42.6 us -> none  [per_device(): lax.psum((gain_attn_part, gain_mlp_part), ('dp', 'mp'))]
    convert_element_type x7 -> x0, other arithmetic: 24.2 us -> none  [the longest x1 10.4 us: per_device(): (probabilities * (grad_probs - inner_sum)).astype(jnp.bfloat16)]
    reduce_sum x7 -> x0, other arithmetic: 11.8 us -> none  [the longest x2 5.82 us: per_device(): row_total = jnp.sum(weights, axis=-1, keepdims=True)]
  transfers between devices with their start and end apart: 9 -> 6, of which waited for: 9 -> 4; matrix products, arithmetic and copies ran while one was open for 8% -> 1% of each run, Pallas kernels for 0% -> 0%
where the time goes in v2:
time: 564 us
  waiting for transfers between devices  313 us (55%)
  Pallas kernels  217 us (38%)
  local copies, waits for them, and re-layouts  15.6 us (3%)
  between operations  13.8 us (2%)
    reduce_scatter x2, waiting for transfers between devices, spread_grads(): lax.psum_scatter(grads, ('col', 'pair'), scatter_dimension=0, tiled=True)  252 us
    pallas_call x1, Pallas kernels, forward_call(): pl.pallas_call(functools.partial(forward_kernel, lengths.shape[1]), out_s...  137 us
    pallas_call x1, Pallas kernels, backward_call(): pl.pallas_call(functools.partial(backward_kernel, bits), out_shape=[jax.S...  80.7 us
    all_gather x2, waiting for transfers between devices, spread_grads(): return lax.all_gather(piece, ('col', 'core'), axis=0, tiled=True)  60.6 us
  transfers between devices with their start and end apart: 6, of which 4 were waited for; matrix products, arithmetic and copies ran while one was open for 1% of the time, Pallas kernels for 0%

profile of v2, /device:TPU:0, one launch (start us, length us, event | category | flops | bytes accessed | tf_op | source)
XLA Modules:
  0.0 563.5 jit_solution(11450137568937251585)
XLA Ops:
  7.2 0.0 reduce-scatter.3.cloned.1.call-start
  7.2 136.7 %forward.1 = (bf16[3,4,4,256,64]{4,3,2,1,0:T(8,128)(2,1)}, bf16[4,256,256]{2,1,0:T(8,128)(2,1)}, bf16[4,256,256]{2,1,0:T(8,128)(2,1)}, f32[4,8,256]{2,1,0:T(8,12...) custom-call(bf16[256,1024]{1,0:T(8,128)(2,1)} %x_own.1, ...), custom_call_target="tpu_custom_call" | custom-call | tf_op jit(solution)/shard_map/forward/pallas_call | solution.py:600
  143.9 80.7 %backward.1 = (bf16[256,1024]{1,0:T(8,128)(2,1)}, f32[256,1024]{1,0:T(8,128)}, bf16[4096,256]{1,0:T(8,128)(2,1)}, f32[8,1024]{1,0:T(8,128)}) custom-call(bf16[3,4,4,256,64]{4,3,2,1,0:T(8,128)(2,1)} %get-tuple-element.26.heads_in, bf16[4,256,256]{2,1,0:T(8,128)(2,1)} %get-tuple-element.27.keys_t, bf16[4,256,256]{2,1,0:T(8,128)(2,1)} %get-tuple-element.28.att_t, ...), custom_call_target="tpu_custom_call" | custom-call | tf_op jit(solution)/shard_map/backward/pallas_call | solution.py:858
  224.7 0.0 reduce-scatter.3.cloned.1.call-update
  224.7 0.0 reduce-scatter.5.cloned.1.call-start
  224.7 0.7 reduce-scatter.5.cloned.1.call-update
  225.4 0.0 all-gather.3.cloned.1.call-start
  225.5 85.6 %reduce-scatter.3.cloned.1.call-done = bf16[512,256]{1,0:T(8,128)(2,1)} async-done(((bf16[4096,256]{1,0:T(8,128)(2,1)}), bf16[512,256]{1,0:T(8,128)(2,1)}) %reduce-scatter.3.cloned.1.call-update) | async-done | bytes 262160 | tf_op jit(solution)/shard_map/reduce_scatter | solution.py:888
  311.1 1.6 collective-permute-start
  312.7 0.0 collective-permute-done
  312.7 0.0 copy-start.4
  312.7 0.7 copy-done.4
  313.4 0.0 all-gather.3.cloned.1.call-update
  313.4 0.0 all-gather.5.cloned.1.call-start
  313.5 166.2 %reduce-scatter.5.cloned.1.call-done = bf16[256,1024]{1,0:T(8,128)(2,1)} async-done(((bf16[2048,1024]{1,0:T(8,128)(2,1)}), bf16[256,1024]{1,0:T(8,128)(2,1)}) %reduce-scatter.5.cloned.1.call-update) | async-done | bytes 524304 | tf_op jit(solution)/shard_map/reduce_scatter | solution.py:888
  479.7 1.7 collective-permute-start.1
  481.4 0.0 collective-permute-done.1
  481.4 0.0 copy-start.3
  481.4 0.8 copy-done.3
  482.2 0.0 all-gather.5.cloned.1.call-update
  482.2 1.4 fusion.1
  483.7 25.8 %all-gather.3.cloned.1.call-done = bf16[4096,256]{1,0:T(8,128)(2,1)} async-done(((bf16[512,256]{1,0:T(8,128)(2,1)}), bf16[4096,256]{1,0:T(8,128)(2,1)}) %all-gather.3.cloned.1.call-update) | async-done | bytes 2097168 | tf_op jit(solution)/shard_map/all_gather | solution.py:895
  509.5 0.0 copy-start
  509.5 1.3 slice.25
  510.8 1.1 copy.18
  511.9 0.0 copy-done
  511.9 1.9 slice.24
  513.8 0.0 copy-start.2
  513.8 0.0 copy-start.1
  513.8 34.8 %all-gather.5.cloned.1.call-done = bf16[2048,1024]{1,0:T(8,128)(2,1)} async-done(((bf16[256,1024]{1,0:T(8,128)(2,1)}), bf16[2048,1024]{1,0:T(8,128)(2,1)}) %all-gather.5.cloned.1.call-update) | async-done | bytes 4194320 | tf_op jit(solution)/shard_map/all_gather | solution.py:895
  548.6 6.7 %fusion = (f32[1024,1024]{1,0:T(8,128)}, f32[1024,1024]{1,0:T(8,128)}) fusion(bf16[2048,1024]{1,0:T(8,128)(2,1)} %all-gather.5.cloned.1.call-done), kind=kLoop, calls=%fused_computation | loop fusion | bytes 16777216 | tf_op jit(solution)/shard_map/slice | solution.py:916
  555.2 0.0 copy-done.2
  555.2 0.8 copy.21
  556.0 0.0 copy-done.1
  556.0 1.0 copy.22
Async XLA Ops:
  7.2 303.9 %reduce-scatter.3.cloned.1.call-start = ((), (), s32[]{:S(2)}) async-start(), calls=%async_computation.2 | async-start | bytes 2359296 | tf_op jit(solution)/shard_map/reduce_scatter | solution.py:888
  224.7 255.0 %reduce-scatter.5.cloned.1.call-start = ((), (), s32[]{:S(2)}) async-start(), calls=%async_computation.4 | async-start | bytes 4718592 | tf_op jit(solution)/shard_map/reduce_scatter | solution.py:888
  225.4 284.1 %all-gather.3.cloned.1.call-start = ((), (), s32[]{:S(2)}) async-start(), calls=%async_computation.3 | async-start | bytes 2359296 | tf_op jit(solution)/shard_map/all_gather | solution.py:895
  311.1 1.6 collective-permute-start
  312.7 0.7 copy-start.4
  313.4 235.1 %all-gather.5.cloned.1.call-start = ((), (), s32[]{:S(2)}) async-start(), calls=%async_computation.5 | async-start | bytes 4718592 | tf_op jit(solution)/shard_map/all_gather | solution.py:895
  479.7 1.7 collective-permute-start.1
  481.4 0.8 copy-start.3
  509.5 2.4 copy-start
  513.8 41.4 %copy-start.2 = (bf16[256,1024]{1,0:T(8,128)(2,1)S(1)}, bf16[256,1024]{1,0:T(8,128)(2,1)}, u32[]{:S(2)}) copy-start(bf16[256,1024]{1,0:T(8,128)(2,1)} %get-tuple-element.56) | copy-start | bytes 1572868
  513.8 42.2 %copy-start.1 = (f32[256,1024]{1,0:T(8,128)S(1)}, f32[256,1024]{1,0:T(8,128)}, u32[]{:S(2)}) copy-start(f32[256,1024]{1,0:T(8,128)} %get-tuple-element.57) | copy-start | bytes 3145732
Sparse Core Ops, SparseCore 0:
  224.8 86.2 reduce-scatter.2
  313.4 166.2 reduce-scatter.4
  482.2 27.2 all-gather.2
  511.8 36.7 all-gather.4

commit v3 on v2

v3 whole, which is shorter than its diff:
```python
import functools
import math

import jax
import jax.numpy as jnp
from jax import lax
from jax.experimental import pallas as pl
from jax.experimental.pallas import tpu as pltpu
from jax.sharding import Mesh
from jax.sharding import PartitionSpec as P

HEAD = 64
EPSILON = 1e-06
NEGATIVE = -1e30
MEMBERS = 4
LOG2E = math.log2(math.e)
GELU_A = math.sqrt(2.0 / math.pi)
GELU_B = 0.044715
AXES = ("col", "core", "pair", "zz")
BF16 = jnp.bfloat16
F32 = jnp.float32
VMEM_LIMIT = 62 << 20
MESH_ID = pl.DeviceIdType.MESH


def dot_nn(a, b):
    return lax.dot_general(a, b, (((1,), (0,)), ((), ())), preferred_element_type=F32)


def dot_nt(a, b):
    return lax.dot_general(a, b, (((1,), (1,)), ((), ())), preferred_element_type=F32)


def dot_tn(a, b):
    return lax.dot_general(a, b, (((0,), (0,)), ((), ())), preferred_element_type=F32)


def flip(bit, amount):
    return bit + amount - 2 * bit * amount


class Place:
    def __init__(self):
        self.col = lax.axis_index("col")
        self.core = lax.axis_index("core")
        self.pair = lax.axis_index("pair")
        self.zz = lax.axis_index("zz")
        self.swapped = self.core != self.pair
        self.stays = self.core == self.pair
        self.me = self.member(0, 0)

    def member(self, other_core, other_chip):
        return 2 * flip(self.core, other_core) + flip(self.zz, other_chip)

    def sibling(self):
        return {"core": 1 - self.core}

    def across(self):
        return {"zz": 1 - self.zz}

    def trade(self):
        return {"pair": 1 - self.pair, "core": 1 - self.core}

    def column(self, bit):
        step = 1 << bit
        here = lax.rem(lax.div(self.col, step), 2)
        return {"col": self.col + step * (1 - 2 * here)}


class Wire:
    def __init__(self, send_sems, recv_sems):
        self.send_sems = send_sems
        self.recv_sems = recv_sems
        self.used = 0

    def copy(self, src, dst, target, got=None):
        number = self.used
        self.used += 1
        return Transfer(
            src, dst, target, dst if got is None else got,
            self.send_sems.at[number], self.recv_sems.at[number],
        )


class Transfer:
    def __init__(self, src, dst, target, got, send_sem, recv_sem):
        self.args = (src, dst, target, got, send_sem, recv_sem)

    def start(self):
        src, dst, target, _, send_sem, recv_sem = self.args
        pltpu.make_async_remote_copy(
            src_ref=src, dst_ref=dst, send_sem=send_sem, recv_sem=recv_sem,
            device_id=target, device_id_type=MESH_ID,
        ).start()

    def wait_send(self):
        src, dst, target, _, send_sem, recv_sem = self.args
        pltpu.make_async_remote_copy(
            src_ref=src, dst_ref=dst, send_sem=send_sem, recv_sem=recv_sem,
            device_id=target, device_id_type=MESH_ID,
        ).wait_send()

    def wait_recv(self):
        _, _, target, got, send_sem, recv_sem = self.args
        pltpu.make_async_remote_copy(
            src_ref=got, dst_ref=got, send_sem=send_sem, recv_sem=recv_sem,
            device_id=target, device_id_type=MESH_ID,
        ).wait_recv()


def meet(targets):
    barrier = pltpu.get_barrier_semaphore()
    for target in targets:
        pl.semaphore_signal(barrier, inc=1, device_id=target, device_id_type=MESH_ID)
    pl.semaphore_wait(barrier, len(targets))


class Gather:
    def __init__(self, wire, place, whole, count=1):
        me, near = place.me, place.member(1, 0)
        far, corner = place.member(0, 1), place.member(1, 1)
        size = whole.shape[1] // count
        self.to_near, self.to_far, self.relay = [], [], []
        for number in range(count):
            at = pl.ds(number * size, size)
            mine, its, across, last = (whole.at[one, at] for one in (me, near, far, corner))
            self.to_near.append(wire.copy(mine, mine, place.sibling(), its))
            self.to_far.append(wire.copy(mine, mine, place.across(), across))
            self.relay.append(wire.copy(across, across, place.sibling(), last))

    def start(self, number=0):
        self.to_far[number].start()
        self.to_near[number].start()

    def take_near(self, number=0):
        self.to_near[number].wait_recv()

    def take_far(self, number=0):
        self.to_far[number].wait_recv()
        self.relay[number].start()

    def take_corner(self, number=0):
        self.relay[number].wait_recv()

    def drain(self):
        for one in self.to_near + self.to_far + self.relay:
            one.wait_send()


class Scatter:
    def __init__(self, wire, place, part, near_in, joined, far_in):
        self.place, self.part = place, part
        self.near_in, self.joined, self.far_in = near_in, joined, far_in
        corner, near = place.member(1, 1), place.member(1, 0)
        self.corner = wire.copy(part.at[corner], near_in.at[0], place.sibling())
        self.near = wire.copy(part.at[near], near_in.at[1], place.sibling())
        self.far = wire.copy(joined, far_in, place.across())

    def send_corner(self):
        self.corner.start()

    def send_near(self):
        self.near.start()

    def send_far(self):
        self.corner.wait_recv()
        far = self.place.member(0, 1)

        def add(at):
            total = self.part[far, at].astype(F32) + self.near_in[0, at].astype(F32)
            self.joined[at] = total.astype(BF16)

        each_rows(self.joined.shape[0], 64, add)
        self.far.start()

    def wait(self):
        self.near.wait_recv()
        self.far.wait_recv()

    def total(self, at):
        return (
            self.part[self.place.me, at].astype(F32)
            + self.near_in[1, at].astype(F32)
            + self.far_in[at].astype(F32)
        )

    def drain(self):
        self.corner.wait_send()
        self.near.wait_send()
        self.far.wait_send()


def window(start, size, unit=16):
    return pl.ds(pl.multiple_of(start, unit), size)


def each_rows(count, size, body):
    def step(number, carry):
        body(window(number * size, size))
        return carry

    lax.fori_loop(0, count // size, step, 0)


def add_rows(count, target, start, one, one_start, two, two_start):
    size = next(size for size in (128, 64, 48, 32, 16) if count % size == 0)

    def step(number, carry):
        moved = number * size
        total = (
            one[window(one_start + moved, size)].astype(F32)
            + two[window(two_start + moved, size)].astype(F32)
        )
        target[window(start + moved, size)] = total.astype(BF16)
        return carry

    lax.fori_loop(0, count // size, step, 0)


class Steps:
    def __init__(self, actions):
        self.actions = list(actions)

    def advance(self):
        if self.actions:
            self.actions.pop(0)()


def advance_all(chains):
    while any(chain.actions for chain in chains):
        for chain in chains:
            chain.advance()


class Reduce(Steps):
    def __init__(self, wire, place, source, start, slots, result, order, local_sem):
        self.place = place
        count, bits = slots.shape[0], len(order)
        here = [lax.rem(lax.div(place.col, 1 << bit), 2) for bit in order]
        offsets = [count - (count >> step) for step in range(bits + 1)]
        piece = count >> bits
        sends, keeps = [], []
        view, view_start = source, start
        for step, bit in enumerate(order):
            half = count >> (step + 1)
            away = view_start + (1 - here[step]) * half
            slot = slots.at[pl.ds(offsets[step], half)]
            sends.append(wire.copy(view.at[window(away, half)], slot, place.column(bit)))
            keeps.append((half, offsets[step], view, view_start + here[step] * half))
            view, view_start = slots, offsets[step]
        final = offsets[bits]
        last = pl.ds(offsets[bits - 1], piece)
        move = wire.copy(slots.at[last], slots.at[pl.ds(final, piece)], {"pair": 1 - place.pair})
        low = jnp.int32(0)
        for step in range(bits):
            low = low + here[step] * (count >> (step + 1))
        owned = result.at[window(low, piece)]
        keep_local = pltpu.make_async_copy(slots.at[pl.ds(final, piece)], owned, local_sem)
        shares = [wire.copy(slots.at[pl.ds(final, piece)], owned, place.sibling())]
        grows = []
        for step in reversed(range(bits)):
            size = count >> (step + 1)
            mine = result.at[window(low, size)]
            other_low = low + (1 - 2 * here[step]) * size
            other = result.at[window(other_low, size)]
            grows.append(wire.copy(mine, mine, place.column(order[step]), other))
            shares.append(wire.copy(other, other, place.sibling()))
            low = low - here[step] * size

        def stays(action):
            pl.when(place.stays)(action)

        def swapped(action):
            pl.when(place.swapped)(action)

        def gather_half(step):
            size, offset, view, start = keeps[step]
            sends[step].wait_recv()
            add_rows(size, slots, offset, slots, offset, view, start)

        def narrow(step):
            gather_half(step)
            sends[step + 1].start()

        def cross():
            gather_half(bits - 1)
            swapped(move.start)

        def settle():
            @stays
            def _():
                move.wait_recv()
                add_rows(piece, slots, final, slots, final, slots, offsets[bits - 1])
                keep_local.start()
                shares[0].start()
                keep_local.wait()
                grows[0].start()

        def widen(step):
            @stays
            def _():
                grows[step].wait_recv()
                if step + 1 < bits:
                    grows[step + 1].start()
                shares[step + 1].start()

        actions = [sends[0].start]
        actions += [functools.partial(narrow, step) for step in range(bits - 1)]
        actions += [cross, settle]
        actions += [functools.partial(widen, step) for step in range(bits)]
        super().__init__(actions)

        def finish():
            for one in sends:
                one.wait_send()

            @swapped
            def _():
                move.wait_send()
                for share in shares:
                    share.wait_recv()

            @stays
            def _():
                for one in grows + shares:
                    one.wait_send()

        self.finish = finish


class Weight:
    def __init__(self, wire, place, source, target, axis, start, size, order, local_sem):
        quarter = lax.rem(place.col, MEMBERS)
        if order[0] == 1:
            quarter = 2 * lax.rem(quarter, 2) + lax.div(quarter, 2)
        depth = size // MEMBERS

        def cut(ref, first, many):
            at = window(start + first, many)
            return ref.at[:, at] if axis == 1 else ref.at[at]

        other = quarter + 1 - 2 * lax.rem(quarter, 2)
        duo = lax.div(quarter, 2)
        mine = cut(target, quarter * depth, depth)
        both = cut(target, duo * 2 * depth, 2 * depth)
        rest = cut(target, (1 - duo) * 2 * depth, 2 * depth)
        self.moves = [
            wire.copy(cut(source, quarter * depth, depth), mine, place.trade()),
            wire.copy(mine, mine, place.column(order[0]), cut(target, other * depth, depth)),
            wire.copy(both, both, place.column(order[1]), rest),
        ]
        self.local = pltpu.make_async_copy(cut(source, 0, size), cut(target, 0, size), local_sem)

    def bring(self):
        self.moves[0].start()

    def pass_on(self, step):
        self.moves[step].wait_recv()
        self.moves[step + 1].start()

    def ready(self):
        self.moves[2].wait_recv()

    def drain(self):
        for one in self.moves:
            one.wait_send()


def scatter_shapes(rows, width):
    return [
        pltpu.VMEM((MEMBERS, rows, width), BF16),
        pltpu.VMEM((2, rows, width), BF16),
        pltpu.VMEM((rows, width), BF16),
        pltpu.VMEM((rows, width), BF16),
    ]


def visible_tile(first_ref, block, tile, rows):
    key_at = tile * rows + lax.broadcasted_iota(jnp.int32, (rows, rows), 0)
    query_at = block * rows + lax.broadcasted_iota(jnp.int32, (rows, rows), 1)
    first = first_ref[0:1, pl.ds(pl.multiple_of(block * rows, rows), rows)]
    return (key_at >= first) & (key_at <= query_at)


def swap_order(step):
    return lax.rem(step, 2), lax.div(step, 2)


def layer_kernel(
    items,
    bits,
    x_own, dy_own, lengths, gain_attn, gain_mlp, wq, wa, wi, wo,
    output, grad_frames, mlp_sums, attn_sums, gains_out,
    wq_m, wa_m, wi_m, wo_m,
    x_all, x_keep, dy_all, normed, normed_mlp, active, grad_hidden,
    qkv, keys_t, values_t, att_t, acc_t, lse, first, first_near, scores,
    part, near, joined, far_in, outs, near2, joined2, far2,
    resid, grad_resid, mlp_grads, mlp_slots, attn_grads, attn_slots, wa_slots,
    projected, gain_sum, gain_got, moved, moved_in, out_keep, out_in,
    send_sems, recv_sems, local_sems,
):
    place = Place()
    wire = Wire(send_sems, recv_sems)
    rows, width = x_keep.shape
    heads = qkv.shape[1]
    features = heads * HEAD
    me = place.me
    frame_count = MEMBERS * rows
    hidden_units = wi.shape[1]
    span = 256
    shift = (HEAD ** -0.5) * LOG2E
    scaling = HEAD ** -0.5
    near_member = place.member(1, 0)

    def when_swapped(action):
        pl.when(place.swapped)(action)

    def when_stays(action):
        pl.when(place.stays)(action)

    chunks = 2
    half = rows // chunks
    x_trades = []
    for number in range(chunks):
        at = pl.ds(number * half, half)
        x_trades.append(
            wire.copy(x_own.at[at], x_all.at[near_member, at], place.trade(), x_all.at[me, at])
        )
    dy_trade = wire.copy(dy_own, dy_all.at[near_member], place.trade(), dy_all.at[me])
    first_trade = wire.copy(first_near.at[0], first_near.at[1], place.sibling())
    x_local = pltpu.make_async_copy(x_own, x_all.at[me], local_sems.at[0])
    dy_local = pltpu.make_async_copy(dy_own, dy_all.at[me], local_sems.at[1])

    def weight(number, source, target, axis, start, size, order):
        return Weight(
            wire, place, source, target, axis, start, size, order, local_sems.at[2 + number]
        )

    part_units = wi.shape[0] // 2
    wq_part = weight(0, wq, wq_m, 1, 0, width, (0, 1))
    wa_part = weight(1, wa, wa_m, 0, 0, features, (1, 0))
    wi_parts = [
        weight(2 + n, wi, wi_m, 0, n * part_units, part_units, (n, 1 - n)) for n in range(2)
    ]
    part_units = wo.shape[0] // 2
    wo_parts = [
        weight(4 + n, wo, wo_m, 0, n * part_units, part_units, (n, 1 - n)) for n in range(2)
    ]
    weights = [wq_part, wa_part] + wi_parts + wo_parts

    meet(
        [place.sibling(), place.across(), place.trade(), {"pair": 1 - place.pair}]
        + [place.column(bit) for bit in range(bits)]
    )

    when_swapped(wq_part.bring)

    @when_stays
    def _():
        x_local.start()
        dy_local.start()
        for one in weights:
            one.local.start()

    position = lax.broadcasted_iota(jnp.int32, (8, frame_count), 1)
    begin = jnp.zeros((8, frame_count), jnp.int32)
    end = jnp.int32(0)
    for item in range(items):
        size = lengths[0, item]
        end = end + size
        begin = begin + jnp.where(position >= end, size, 0)
    first_near[0] = jnp.where(position >= end, position, begin)
    first_trade.start()

    gather_x = Gather(wire, place, x_all, chunks)
    gather_dy = Gather(wire, place, dy_all)
    gather_n = Gather(wire, place, normed_mlp)
    grad_all = x_all
    gather_g = Gather(wire, place, grad_all)

    @when_swapped
    def _():
        wq_part.pass_on(0)
        for one in x_trades:
            one.start()
        wq_part.pass_on(1)
        for number in range(chunks):
            x_trades[number].wait_recv()
            gather_x.start(number)
        wa_part.bring()
        dy_trade.start()

    @when_stays
    def _():
        x_local.wait()
        for number in range(chunks):
            gather_x.start(number)

    gain = gain_attn[...]

    def norm_block(member):
        def some(at):
            values = x_all[member, at].astype(F32)
            scale = lax.rsqrt(jnp.mean(values * values, axis=-1, keepdims=True) + EPSILON)
            normed[member, at] = (values * scale * gain).astype(BF16)

        each_rows(rows, 64, some)

    def project(member):
        source = normed[member]
        for kind in range(3):
            block = dot_nn(source, wq_m[kind])
            narrow = block.astype(BF16)
            for head in range(heads):
                qkv[kind, head, member] = narrow[:, head * HEAD : (head + 1) * HEAD]
            if kind == 1:
                keys_t[member] = block.T.astype(BF16)
            if kind == 2:
                values_t[member] = block.T.astype(BF16)

    def arrive(step, carry):
        member = place.member(*swap_order(step))

        @pl.when(step == 1)
        def _():
            for number in range(chunks):
                gather_x.take_near(number)

        @pl.when(step == 2)
        def _():
            for number in range(chunks):
                gather_x.take_far(number)

        @pl.when(step == 3)
        def _():
            for number in range(chunks):
                gather_x.take_corner(number)

        norm_block(member)

        @pl.when(step == 0)
        def _():
            when_swapped(wq_part.ready)
            when_stays(wq_part.local.wait)

        @pl.when((step == 2) & place.swapped)
        def _():
            wa_part.pass_on(0)

        project(member)
        return carry

    lax.fori_loop(0, MEMBERS, arrive, 0)
    x_keep[...] = x_all[me]
    first_trade.wait_recv()

    @when_swapped
    def _():
        first[...] = first_near[1]
        wa_part.pass_on(1)
        dy_trade.wait_recv()
        for one in wi_parts:
            one.bring()

    @when_stays
    def _():
        first[...] = first_near[0]
        dy_local.wait()
        wa_part.local.wait()

    gather_dy.start()
    scatter1 = Scatter(wire, place, part, near, joined, far_in)

    def attend(step, carry):
        block = place.member(*swap_order(3 - step))

        def score(tile, peaks):
            seen = visible_tile(first, block, tile, rows)
            higher = []
            for head in range(heads):
                raw = dot_nt(qkv[1, head, tile], qkv[0, head, block])
                raw = jnp.where(seen, raw, NEGATIVE)
                scores[head, tile] = raw
                higher.append(jnp.maximum(peaks[head], jnp.max(raw, axis=0, keepdims=True)))
            return tuple(higher)

        low = jnp.full((1, rows), NEGATIVE, F32)
        peaks = lax.fori_loop(0, block + 1, score, (low,) * heads)
        acc_t[...] = jnp.zeros_like(acc_t)

        def weigh(tile, totals):
            sums = []
            for head in range(heads):
                prob = jnp.exp2((scores[head, tile] - peaks[head]) * shift)
                sums.append(totals[head] + jnp.sum(prob, axis=0, keepdims=True))
                at = slice(head * HEAD, (head + 1) * HEAD)
                acc_t[at] += dot_nn(values_t[tile, at], prob.astype(BF16))
            return tuple(sums)

        none = jnp.zeros((1, rows), F32)
        totals = lax.fori_loop(0, block + 1, weigh, (none,) * heads)
        for head in range(heads):
            at = slice(head * HEAD, (head + 1) * HEAD)
            acc_t[at] = acc_t[at] / totals[head]
            lse[block, head : head + 1] = peaks[head] * shift + jnp.log2(totals[head])
        att_t[block] = acc_t[...].astype(BF16)

        @pl.when((step == 0) & place.swapped)
        def _():
            wa_part.ready()

        attended = acc_t[...].T.astype(BF16)
        part[block] = dot_nn(attended, wa_m[...]).astype(BF16)

        @pl.when(step == 0)
        def _():
            scatter1.send_corner()

        @pl.when(step == 1)
        def _():
            scatter1.send_far()

            @when_swapped
            def _():
                wi_parts[0].pass_on(0)
                wo_parts[0].bring()

        @pl.when(step == 2)
        def _():
            scatter1.send_near()

        @pl.when((step == 3) & place.swapped)
        def _():
            wi_parts[1].pass_on(0)
            wo_parts[1].bring()

        return carry

    lax.fori_loop(0, MEMBERS, attend, 0)

    gather_dy.take_near()
    gather_dy.take_far()

    @when_swapped
    def _():
        for one in wi_parts:
            one.pass_on(1)
        for one in wo_parts:
            one.pass_on(0)

    scatter1.wait()
    gain2 = gain_mlp[...]

    def add_resid(at):
        total = x_keep[at].astype(F32) + scatter1.total(at)
        resid[at] = total
        scale = lax.rsqrt(jnp.mean(total * total, axis=-1, keepdims=True) + EPSILON)
        normed_mlp[me, at] = (total * scale * gain2).astype(BF16)

    each_rows(rows, 64, add_resid)
    gather_n.start()
    gather_x.drain()
    scatter1.drain()

    @when_swapped
    def _():
        for one in wo_parts:
            one.pass_on(1)
        for one in wi_parts + wo_parts:
            one.ready()

    @when_stays
    def _():
        for one in wi_parts + wo_parts:
            one.local.wait()

    gather_dy.take_corner()
    scatter3 = Scatter(wire, place, part, near, joined, far_in)

    def feed(step, carry):
        flip_core = jnp.where((step == 1) | (step == 2), 1, 0)
        flip_chip = jnp.where(step >= 2, 1, 0)
        block = place.member(flip_core, flip_chip)

        @pl.when(step == 1)
        def _():
            gather_n.take_near()

        @pl.when(step == 2)
        def _():
            gather_n.take_far()
            gather_n.take_corner()

        def units(number, inner):
            at = pl.ds(pl.multiple_of(number * span, span), span)
            hidden = dot_nn(normed_mlp[block], wi_m[:, at])
            grad_active = dot_nt(dy_all[block], wo_m[at])
            square = hidden * hidden
            bend = jnp.tanh(GELU_A * hidden * (1.0 + GELU_B * square))
            upper = 0.5 * (1.0 + bend)
            active[block, :, at] = (hidden * upper).astype(BF16)
            slope = upper + 0.5 * hidden * (1.0 - bend * bend) * (
                GELU_A * (1.0 + 3.0 * GELU_B * square)
            )
            grad_hidden[block, :, at] = (grad_active * slope).astype(BF16)
            return inner

        lax.fori_loop(0, hidden_units // span, units, 0)

        def across_features(number, inner):
            at = pl.ds(pl.multiple_of(number * span, span), span)
            part[block, :, at] = dot_nt(grad_hidden[block], wi_m[at]).astype(BF16)
            outs[block, :, at] = dot_nn(active[block], wo_m[:, at]).astype(BF16)
            return inner

        lax.fori_loop(0, width // span, across_features, 0)

        @pl.when(step == 1)
        def _():
            scatter3.send_near()

        @pl.when(step == 2)
        def _():
            scatter3.send_corner()

        @pl.when(step == 3)
        def _():
            scatter3.send_far()

        return carry

    lax.fori_loop(0, MEMBERS, feed, 0)

    ahead, back = tuple(range(bits)), tuple(reversed(range(bits)))
    sum_in = Reduce(
        wire, place, mlp_grads, 0, mlp_slots.at[pl.ds(0, width)],
        mlp_sums.at[pl.ds(0, width)], ahead, local_sems.at[8],
    )
    sum_out = Reduce(
        wire, place, mlp_grads, width, mlp_slots.at[pl.ds(width, hidden_units)],
        mlp_sums.at[pl.ds(width, hidden_units)], back, local_sems.at[9],
    )
    split = 3 * width // 2
    sum_one = Reduce(
        wire, place, attn_grads, 0, attn_slots.at[pl.ds(0, split)],
        attn_sums.at[pl.ds(0, split)], ahead, local_sems.at[10],
    )
    sum_two = Reduce(
        wire, place, attn_grads, split, attn_slots.at[pl.ds(split, split)],
        attn_sums.at[pl.ds(split, split)], back, local_sems.at[11],
    )
    sum_proj = Reduce(
        wire, place, attn_grads, 3 * width, wa_slots,
        attn_sums.at[pl.ds(3 * width, width)], ahead, local_sems.at[12],
    )

    def in_grads(number, carry):
        at = pl.ds(pl.multiple_of(number * span, span), span)
        left = normed_mlp[:, :, at].reshape(frame_count, span)
        right = grad_hidden[...].reshape(frame_count, hidden_units)
        mlp_grads[at] = dot_tn(left, right).astype(BF16)
        return carry

    def out_grads(number, carry):
        at = pl.ds(pl.multiple_of(number * span, span), span)
        down = pl.ds(pl.multiple_of(width + number * span, span), span)
        left = active[:, :, at].reshape(frame_count, span)
        right = dy_all[...].reshape(frame_count, width)
        mlp_grads[down] = dot_tn(left, right).astype(BF16)
        return carry

    lax.fori_loop(0, width // span, in_grads, 0)
    sum_in.advance()
    lax.fori_loop(0, hidden_units // span, out_grads, 0)
    sum_out.advance()

    scatter3.wait()
    gain_sum[...] = jnp.zeros_like(gain_sum)

    def norm_back(at):
        grad = scatter3.total(at)
        values = resid[at]
        scale = lax.rsqrt(jnp.mean(values * values, axis=-1, keepdims=True) + EPSILON)
        gain_sum[0:1] += jnp.sum(grad * values * scale, axis=0, keepdims=True)
        scaled = grad * gain2
        mean = jnp.mean(scaled * values, axis=-1, keepdims=True)
        total = (
            dy_all[me, at].astype(F32) + scale * scaled - values * (scale * scale * scale) * mean
        )
        grad_resid[at] = total
        grad_all[me, at] = total.astype(BF16)

    each_rows(rows, 64, norm_back)
    gather_g.start()
    scatter3.drain()
    scatter2 = Scatter(wire, place, outs, near2, joined2, far2)
    scatter2.send_corner()
    scatter2.send_near()
    scores[...] = jnp.zeros_like(scores)

    def block_back(step, carry):
        block = place.member(*swap_order(step))

        @pl.when(step == 1)
        def _():
            gather_g.take_near()

        @pl.when(step == 2)
        def _():
            gather_g.take_far()
            scatter2.send_far()
            sum_in.advance()

        @pl.when(step == 3)
        def _():
            sum_out.advance()
            gather_g.take_corner()

        source = grad_all[block]
        top = dot_nt(source, wa_m[...]).astype(BF16)
        turned = dot_nt(wa_m[...], source).astype(BF16)
        tops = [top[:, head * HEAD : (head + 1) * HEAD] for head in range(heads)]
        product = turned.astype(F32) * att_t[block].astype(F32)
        deltas = [
            jnp.sum(product[head * HEAD : (head + 1) * HEAD], axis=0, keepdims=True)
            for head in range(heads)
        ]
        acc_t[...] = jnp.zeros_like(acc_t)

        def tiles(tile, inner):
            seen = visible_tile(first, block, tile, rows)
            for head in range(heads):
                at = slice(head * HEAD, (head + 1) * HEAD)
                query = qkv[0, head, block]
                raw = dot_nt(qkv[1, head, tile], query)
                prob = jnp.where(
                    seen, jnp.exp2(raw * shift - lse[block, head : head + 1]), 0.0
                )
                grad_prob = dot_nt(qkv[2, head, tile], tops[head])
                grad_score = (prob * (grad_prob - deltas[head])).astype(BF16)
                scores[head, tile, :, 128 : 128 + HEAD] += dot_nn(prob.astype(BF16), tops[head])
                scores[head, tile, :, 0:HEAD] += dot_nn(grad_score, query)
                acc_t[at] += dot_nn(keys_t[tile, at], grad_score)
            return inner

        lax.fori_loop(0, block + 1, tiles, 0)
        projected[0, block] = (acc_t[...].T * scaling).astype(BF16)
        return carry

    lax.fori_loop(0, MEMBERS, block_back, 0)

    def settle_heads(block, carry):
        for head in range(heads):
            at = slice(head * HEAD, (head + 1) * HEAD)
            grad_keys = scores[head, block, :, 0:HEAD] * scaling
            projected[1, block, :, at] = grad_keys.astype(BF16)
            projected[2, block, :, at] = scores[head, block, :, 128 : 128 + HEAD].astype(BF16)
        return carry

    lax.fori_loop(0, MEMBERS, settle_heads, 0)

    for kind in range(3):

        def qkv_grads(number, carry, kind=kind):
            at = pl.ds(pl.multiple_of(number * span, span), span)
            to = pl.ds(pl.multiple_of(kind * width + number * span, span), span)
            left = normed[:, :, at].reshape(frame_count, span)
            right = projected[kind].reshape(frame_count, features)
            attn_grads[to] = dot_tn(left, right).astype(BF16)
            return carry

        lax.fori_loop(0, width // span, qkv_grads, 0)

    sum_one.advance()
    sum_two.advance()
    scatter4 = Scatter(wire, place, part, near, joined, far_in)

    def inputs_back(step, carry):
        block = place.member(*swap_order(3 - step))

        def columns(number, inner):
            down = pl.ds(pl.multiple_of(number * span, span), span)
            total = dot_nt(projected[0, block], wq_m[0, down])
            total += dot_nt(projected[1, block], wq_m[1, down])
            total += dot_nt(projected[2, block], wq_m[2, down])
            part[block, :, down] = total.astype(BF16)
            return inner

        lax.fori_loop(0, width // span, columns, 0)

        @pl.when(step == 0)
        def _():
            scatter4.send_corner()

        @pl.when(step == 1)
        def _():
            scatter4.send_far()

        @pl.when(step == 2)
        def _():
            scatter4.send_near()

        return carry

    lax.fori_loop(0, MEMBERS, inputs_back, 0)

    def proj_grads(number, carry):
        at = pl.ds(pl.multiple_of(number * features, features), features)
        to = pl.ds(pl.multiple_of(3 * width + number * features, features), features)
        total = dot_nn(att_t[0], grad_all[0, :, at])
        for member in range(1, MEMBERS):
            total += dot_nn(att_t[member], grad_all[member, :, at])
        attn_grads[to] = total.astype(BF16)
        return carry

    lax.fori_loop(0, width // features, proj_grads, 0)
    sum_proj.advance()
    sum_in.advance()
    scatter2.wait()

    def finish_output(at):
        out_keep[at] = (resid[at] + scatter2.total(at)).astype(BF16)

    each_rows(rows, 64, finish_output)
    out_trade = wire.copy(out_keep, out_in, place.trade())
    when_swapped(out_trade.start)
    sum_out.advance()
    sum_one.advance()
    sum_two.advance()
    sum_proj.advance()

    scatter4.wait()

    def finish_frames(at):
        grad = scatter4.total(at)
        values = x_keep[at].astype(F32)
        scale = lax.rsqrt(jnp.mean(values * values, axis=-1, keepdims=True) + EPSILON)
        gain_sum[1:2] += jnp.sum(grad * values * scale, axis=0, keepdims=True)
        scaled = grad * gain
        mean = jnp.mean(scaled * values, axis=-1, keepdims=True)
        total = grad_resid[at] + scale * scaled - values * (scale * scale * scale) * mean
        grad_frames[at] = total
        moved[at] = total.astype(BF16)

    each_rows(rows, 64, finish_frames)
    frames_trade = wire.copy(moved, moved_in, place.trade())
    when_swapped(frames_trade.start)

    partners = [place.sibling(), place.across(), {"pair": 1 - place.pair}]
    partners += [place.column(bit) for bit in range(bits)]
    gain_trades = [
        wire.copy(gain_sum.at[pl.ds(8 * number, 8)], gain_got.at[number], partner)
        for number, partner in enumerate(partners)
    ]

    def gain_step(number):
        gain_trades[number].wait_recv()
        here = slice(8 * number, 8 * number + 8)
        gain_sum[8 * number + 8 : 8 * number + 16] = gain_sum[here] + gain_got[number]
        if number + 1 < len(gain_trades):
            gain_trades[number + 1].start()

    gain_trades[0].start()
    gain_chain = Steps([functools.partial(gain_step, n) for n in range(len(partners))])
    sums = [sum_one, sum_two, sum_proj, sum_in, sum_out]
    advance_all([gain_chain] + sums)
    gains_out[...] = gain_sum[8 * len(partners) : 8 * len(partners) + 8]

    @when_swapped
    def _():
        out_trade.wait_recv()
        output[...] = out_in[...]
        frames_trade.wait_recv()
        grad_frames[...] = moved_in[...].astype(F32)
        out_trade.wait_send()
        frames_trade.wait_send()
        for one in x_trades + [dy_trade]:
            one.wait_send()
        for one in weights:
            one.drain()

    @when_stays
    def _():
        output[...] = out_keep[...]

    for one in (gather_dy, gather_n, gather_g, scatter2, scatter4):
        one.drain()
    first_trade.wait_send()
    for one in gain_trades:
        one.wait_send()
    for one in sums:
        one.finish()


def layer_call(bits, x_own, dy_own, lengths, gain_attn, gain_mlp, wq, wa, wi, wo):
    rows, width = x_own.shape
    features = wa.shape[0]
    heads = features // HEAD
    units = wi.shape[1]
    frames = MEMBERS * rows
    steps = 3 + bits
    members = (MEMBERS, rows, width)
    block = pl.BlockSpec(memory_space=pltpu.VMEM)
    whole = pl.BlockSpec(memory_space=pl.ANY)
    outputs = [
        ((rows, width), BF16, block),
        ((rows, width), F32, block),
        ((width + units, width), BF16, whole),
        ((4 * width, features), BF16, whole),
        ((8, width), F32, block),
    ]
    scratch = [
        (wq.shape, BF16),
        (wa.shape, BF16),
        (wi.shape, BF16),
        (wo.shape, BF16),
        (members, BF16),
        ((rows, width), BF16),
        (members, BF16),
        (members, BF16),
        (members, BF16),
        ((MEMBERS, rows, units), BF16),
        ((MEMBERS, rows, units), BF16),
        ((3, heads, MEMBERS, rows, HEAD), BF16),
        ((MEMBERS, features, rows), BF16),
        ((MEMBERS, features, rows), BF16),
        ((MEMBERS, features, rows), BF16),
        ((features, rows), F32),
        ((MEMBERS, 8, rows), F32),
        ((8, frames), jnp.int32),
        ((2, 8, frames), jnp.int32),
        ((heads, MEMBERS, rows, rows), F32),
    ]
    scatter = [(members, BF16), ((2, rows, width), BF16), ((rows, width), BF16),
               ((rows, width), BF16)]
    scratch += scatter * 2
    scratch += [
        ((rows, width), F32),
        ((rows, width), F32),
        ((width + units, width), BF16),
        ((width + units, width), BF16),
        ((4 * width, features), BF16),
        ((3 * width, features), BF16),
        ((width, features), BF16),
        ((3, MEMBERS, rows, features), BF16),
        ((8 * steps + 8, width), F32),
        ((steps, 8, width), F32),
    ]
    scratch += [((rows, width), BF16)] * 4
    count = 64 + 5 * (3 * bits + 2)
    return pl.pallas_call(
        functools.partial(layer_kernel, lengths.shape[1], bits),
        out_shape=[jax.ShapeDtypeStruct(shape, kind) for shape, kind, _ in outputs],
        in_specs=[whole, whole, pl.BlockSpec(memory_space=pltpu.SMEM), block, block]
        + [whole] * 4,
        out_specs=[spec for _, _, spec in outputs],
        scratch_shapes=[pltpu.VMEM(shape, kind) for shape, kind in scratch]
        + [
            pltpu.SemaphoreType.DMA((count,)),
            pltpu.SemaphoreType.DMA((count,)),
            pltpu.SemaphoreType.DMA((13,)),
        ],
        compiler_params=pltpu.CompilerParams(
            collective_id=0, has_side_effects=True, vmem_limit_bytes=VMEM_LIMIT
        ),
        name="layer",
    )(x_own, dy_own, lengths, gain_attn, gain_mlp, wq, wa, wi, wo)


def per_device(bits, frames, lengths, wq, wa, wi, wo, gain_attn, gain_mlp, cotangent):
    width = frames.shape[1]
    features = wa.shape[0]
    output, grad_frames, mlp_sums, attn_sums, gains = layer_call(
        bits, frames, cotangent, lengths, gain_attn.reshape(1, width),
        gain_mlp.reshape(1, width), wq, wa, wi, wo,
    )
    mlp_sums = mlp_sums.astype(F32)
    attn_sums = attn_sums.astype(F32)
    grad_wq = attn_sums[: 3 * width].reshape(3, width, features)
    turned = attn_sums[3 * width :].reshape(width // features, features, features)
    grad_wa = jnp.transpose(turned, (1, 0, 2)).reshape(features, width)
    return (
        output,
        grad_frames,
        grad_wq,
        grad_wa,
        mlp_sums[:width],
        mlp_sums[width:],
        gains[1],
        gains[0],
    )


def solution(mesh):
    batches = mesh.shape["dp"]
    bits = (batches // 2).bit_length() - 1
    inner = Mesh(mesh.devices.reshape(batches // 2, 2, 2, 2), AXES)
    dp, mp = ("col", "core"), ("pair", "zz")
    rows = P(dp + mp, None)
    weights = (P(None, None, mp), P(mp, None), P(None, mp), P(mp, None))
    return jax.shard_map(
        functools.partial(per_device, bits),
        mesh=inner,
        in_specs=(rows, P(dp, None)) + weights + (P(), P(), rows),
        out_specs=(rows, rows) + weights + (P(), P()),
        check_vma=False,
    )
```

time: 564 us -> 267 us (0.47)
  waiting for transfers between devices: 313 us -> 0 us
  Pallas kernels: 217 us -> 253 us
  between operations: 13.8 us -> 0.67 us
    reduce_scatter x2 -> x0, waiting for transfers between devices: 252 us -> none  [spread_grads(): lax.psum_scatter(grads, ('col', 'pair'), scatter_dimension=0, tiled=True)]
    all_gather x2 -> x0, waiting for transfers between devices: 60.6 us -> none  [spread_grads(): return lax.all_gather(piece, ('col', 'core'), axis=0, tiled=True)]
    pallas_call x2 -> x1, Pallas kernels: 217 us -> 253 us  [layer_call(): pl.pallas_call(functools.partial(layer_kernel, lengths.shape[1], bits), o...]
  transfers between devices with their start and end apart: 6 -> 0, of which waited for: 4 -> 0; matrix products, arithmetic and copies ran while one was open for 1% -> 0% of each run, Pallas kernels for 0% -> 0%
where the time goes in v3:
time: 267 us; the launch traced here: 266 us
  Pallas kernels  253 us (95%)
  local copies, waits for them, and re-layouts  13.1 us (5%)
    pallas_call x1, Pallas kernels, layer_call(): pl.pallas_call(functools.partial(layer_kernel, lengths.shape[1], bits), o...  253 us
    slice x1, local copies, waits for them, and re-layouts, per_device(): mlp_sums[width:]  6.81 us

profile of v3, /device:TPU:0, one launch (start us, length us, event | category | flops | bytes accessed | tf_op | source)
XLA Modules:
  0.0 266.4 jit_solution(7439892083135789441)
XLA Ops:
  0.6 252.6 %layer.1 = (bf16[256,1024]{1,0:T(8,128)(2,1)}, f32[256,1024]{1,0:T(8,128)}, bf16[2048,1024]{1,0:T(8,128)(2,1)}, bf16[4096,256]{1,0:T(8,128)(2,1)}, f32[8,1024]{1,0:T(8,128)}) custom-call(bf16[256,1024]{1,0:T(8,128)(2,1)} %x_own.1, bf16[256,1024]{1,0:T(8,128)(2,1)} %dy_own.1, s32[1,6]{1,0:T(1,128)} %lengths.1, f32[1,1024]{1,0:T(1,128)} %bitcast.13, ...), custom_call_target="tpu_custom_call" | custom-call | tf_op jit(solution)/shard_map/layer/pallas_call | solution.py:1051
  253.3 0.0 copy-start
  253.3 6.8 %fusion = (f32[1024,1024]{1,0:T(8,128)}, f32[1024,1024]{1,0:T(8,128)}) fusion(bf16[2048,1024]{1,0:T(8,128)(2,1)} %get-tuple-element.16), kind=kLoop, calls=%fused_computation | loop fusion | bytes 16777216 | tf_op jit(solution)/shard_map/slice | solution.py:1088
  260.1 0.0 copy-done
  260.1 0.0 copy-start.2
  260.1 1.9 slice.24
  262.0 0.0 copy-start.1
  262.0 0.1 slice.25
  262.1 1.1 copy.18
  263.2 1.4 fusion.1
  264.6 0.0 copy-done.2
  264.6 0.8 copy.21
  265.4 0.0 copy-done.1
  265.4 1.0 copy.22
Async XLA Ops:
  253.3 6.8 %copy-start = (bf16[4096,256]{1,0:T(8,128)(2,1)S(1)}, bf16[4096,256]{1,0:T(8,128)(2,1)}, u32[]{:S(2)}) copy-start(bf16[4096,256]{1,0:T(8,128)(2,1)} %get-tuple-element.15) | copy-start | bytes 6291460
  260.1 4.5 %copy-start.2 = (bf16[256,1024]{1,0:T(8,128)(2,1)S(1)}, bf16[256,1024]{1,0:T(8,128)(2,1)}, u32[]{:S(2)}) copy-start(bf16[256,1024]{1,0:T(8,128)(2,1)} %get-tuple-element.30) | copy-start | bytes 1572868
  262.0 3.4 %copy-start.1 = (f32[256,1024]{1,0:T(8,128)S(1)}, f32[256,1024]{1,0:T(8,128)}, u32[]{:S(2)}) copy-start(f32[256,1024]{1,0:T(8,128)} %get-tuple-element.31) | copy-start | bytes 3145732

commit v4 on v3

--- a/solution.py
+++ b/solution.py
@@ -148,13 +148,17 @@
 
 
 class Scatter:
-    def __init__(self, wire, place, part, near_in, joined, far_in):
+    def __init__(self, wire, place, part, near_in, joined, far_in, count=1):
         self.place, self.part = place, part
         self.near_in, self.joined, self.far_in = near_in, joined, far_in
         corner, near = place.member(1, 1), place.member(1, 0)
         self.corner = wire.copy(part.at[corner], near_in.at[0], place.sibling())
         self.near = wire.copy(part.at[near], near_in.at[1], place.sibling())
-        self.far = wire.copy(joined, far_in, place.across())
+        self.size = joined.shape[0] // count
+        self.far = []
+        for number in range(count):
+            at = pl.ds(number * self.size, self.size)
+            self.far.append(wire.copy(joined.at[at], far_in.at[at], place.across()))
 
     def send_corner(self):
         self.corner.start()
@@ -170,12 +174,17 @@
             total = self.part[far, at].astype(F32) + self.near_in[0, at].astype(F32)
             self.joined[at] = total.astype(BF16)
 
-        each_rows(self.joined.shape[0], 64, add)
-        self.far.start()
-
-    def wait(self):
+        for number, one in enumerate(self.far):
+            each_rows(self.size, 64, add, number * self.size)
+            one.start()
+
+    def finish(self, body, after=None):
         self.near.wait_recv()
-        self.far.wait_recv()
+        for number, one in enumerate(self.far):
+            one.wait_recv()
+            each_rows(self.size, 64, body, number * self.size)
+            if after is not None:
+                after(number)
 
     def total(self, at):
         return (
@@ -187,16 +196,17 @@
     def drain(self):
         self.corner.wait_send()
         self.near.wait_send()
-        self.far.wait_send()
+        for one in self.far:
+            one.wait_send()
 
 
 def window(start, size, unit=16):
     return pl.ds(pl.multiple_of(start, unit), size)
 
 
-def each_rows(count, size, body):
+def each_rows(count, size, body, start=0):
     def step(number, carry):
-        body(window(number * size, size))
+        body(window(start + number * size, size))
         return carry
 
     lax.fori_loop(0, count // size, step, 0)
@@ -256,14 +266,16 @@
             low = low + here[step] * (count >> (step + 1))
         owned = result.at[window(low, piece)]
         keep_local = pltpu.make_async_copy(slots.at[pl.ds(final, piece)], owned, local_sem)
-        shares = [wire.copy(slots.at[pl.ds(final, piece)], owned, place.sibling())]
+        whole = slots.at[pl.ds(final, piece)]
+        shares = [wire.copy(whole, owned, place.sibling())]
         grows = []
         for step in reversed(range(bits)):
             size = count >> (step + 1)
             mine = result.at[window(low, size)]
             other_low = low + (1 - 2 * here[step]) * size
             other = result.at[window(other_low, size)]
-            grows.append(wire.copy(mine, mine, place.column(order[step]), other))
+            held = mine if grows else whole
+            grows.append(wire.copy(held, mine, place.column(order[step]), other))
             shares.append(wire.copy(other, other, place.sibling()))
             low = low - here[step] * size
 
@@ -291,15 +303,16 @@
             def _():
                 move.wait_recv()
                 add_rows(piece, slots, final, slots, final, slots, offsets[bits - 1])
+                grows[0].start()
+                shares[0].start()
                 keep_local.start()
-                shares[0].start()
-                keep_local.wait()
-                grows[0].start()
 
         def widen(step):
             @stays
             def _():
                 grows[step].wait_recv()
+                if step == 0:
+                    keep_local.wait()
                 if step + 1 < bits:
                     grows[step + 1].start()
                 shares[step + 1].start()
@@ -390,12 +403,12 @@
     items,
     bits,
     x_own, dy_own, lengths, gain_attn, gain_mlp, wq, wa, wi, wo,
-    output, grad_frames, mlp_sums, attn_sums, gains_out,
+    output, grad_frames, in_sums, out_sums, qkv_sums, wa_sums, gains_out,
     wq_m, wa_m, wi_m, wo_m,
     x_all, x_keep, dy_all, normed, normed_mlp, active, grad_hidden,
     qkv, keys_t, values_t, att_t, acc_t, lse, first, first_near, scores,
     part, near, joined, far_in, outs, near2, joined2, far2,
-    resid, grad_resid, mlp_grads, mlp_slots, attn_grads, attn_slots, wa_slots,
+    resid, grad_resid, mlp_grads, mlp_slots, attn_grads, attn_slots, wa_grads, wa_slots,
     projected, gain_sum, gain_got, moved, moved_in, out_keep, out_in,
     send_sems, recv_sems, local_sems,
 ):
@@ -407,7 +420,7 @@
     me = place.me
     frame_count = MEMBERS * rows
     hidden_units = wi.shape[1]
-    span = 256
+    span = rows
     shift = (HEAD ** -0.5) * LOG2E
     scaling = HEAD ** -0.5
     near_member = place.member(1, 0)
@@ -436,24 +449,30 @@
             wire, place, source, target, axis, start, size, order, local_sems.at[2 + number]
         )
 
-    part_units = wi.shape[0] // 2
-    wq_part = weight(0, wq, wq_m, 1, 0, width, (0, 1))
-    wa_part = weight(1, wa, wa_m, 0, 0, features, (1, 0))
-    wi_parts = [
-        weight(2 + n, wi, wi_m, 0, n * part_units, part_units, (n, 1 - n)) for n in range(2)
-    ]
-    part_units = wo.shape[0] // 2
-    wo_parts = [
-        weight(4 + n, wo, wo_m, 0, n * part_units, part_units, (n, 1 - n)) for n in range(2)
-    ]
-    weights = [wq_part, wa_part] + wi_parts + wo_parts
+    def halves(number, source, target, axis):
+        size = source.shape[axis] // 2
+        return [
+            weight(number + n, source, target, axis, n * size, size, (n, 1 - n)) for n in range(2)
+        ]
+
+    wq_parts = halves(0, wq, wq_m, 1)
+    wi_parts = halves(2, wi, wi_m, 0)
+    wo_parts = halves(4, wo, wo_m, 0)
+    wa_part = weight(6, wa, wa_m, 0, 0, features, (1, 0))
+    weights = wq_parts + [wa_part] + wi_parts + wo_parts
 
     meet(
         [place.sibling(), place.across(), place.trade(), {"pair": 1 - place.pair}]
         + [place.column(bit) for bit in range(bits)]
     )
 
-    when_swapped(wq_part.bring)
+    @when_swapped
+    def _():
+        for one in wq_parts:
+            one.bring()
+        for one in x_trades:
+            one.start()
+        wa_part.bring()
 
     @when_stays
     def _():
@@ -474,27 +493,28 @@
 
     gather_x = Gather(wire, place, x_all, chunks)
     gather_dy = Gather(wire, place, dy_all)
-    gather_n = Gather(wire, place, normed_mlp)
+    gather_n = Gather(wire, place, normed_mlp, chunks)
     grad_all = x_all
-    gather_g = Gather(wire, place, grad_all)
+    slopes = scores
+    gather_g = Gather(wire, place, grad_all, chunks)
 
     @when_swapped
     def _():
-        wq_part.pass_on(0)
-        for one in x_trades:
-            one.start()
-        wq_part.pass_on(1)
+        for one in wq_parts:
+            one.pass_on(0)
+        for one in wq_parts:
+            one.pass_on(1)
         for number in range(chunks):
             x_trades[number].wait_recv()
             gather_x.start(number)
-        wa_part.bring()
-        dy_trade.start()
 
     @when_stays
     def _():
         x_local.wait()
         for number in range(chunks):
             gather_x.start(number)
+        dy_local.wait()
+        gather_dy.start()
 
     gain = gain_attn[...]
 
@@ -531,6 +551,14 @@
             for number in range(chunks):
                 gather_x.take_far(number)
 
+            @when_swapped
+            def _():
+                for one in wi_parts:
+                    one.bring()
+                dy_trade.start()
+                for one in wo_parts:
+                    one.bring()
+
         @pl.when(step == 3)
         def _():
             for number in range(chunks):
@@ -540,8 +568,9 @@
 
         @pl.when(step == 0)
         def _():
-            when_swapped(wq_part.ready)
-            when_stays(wq_part.local.wait)
+            for one in wq_parts:
+                when_swapped(one.ready)
+                when_stays(one.local.wait)
 
         @pl.when((step == 2) & place.swapped)
         def _():
@@ -558,18 +587,13 @@
     def _():
         first[...] = first_near[1]
         wa_part.pass_on(1)
-        dy_trade.wait_recv()
-        for one in wi_parts:
-            one.bring()
 
     @when_stays
     def _():
         first[...] = first_near[0]
-        dy_local.wait()
         wa_part.local.wait()
 
-    gather_dy.start()
-    scatter1 = Scatter(wire, place, part, near, joined, far_in)
+    scatter1 = Scatter(wire, place, part, near, joined, far_in, chunks)
 
     def attend(step, carry):
         block = place.member(*swap_order(3 - step))
@@ -580,7 +604,7 @@
             for head in range(heads):
                 raw = dot_nt(qkv[1, head, tile], qkv[0, head, block])
                 raw = jnp.where(seen, raw, NEGATIVE)
-                scores[head, tile] = raw
+                scores[tile, :, head * rows : (head + 1) * rows] = raw
                 higher.append(jnp.maximum(peaks[head], jnp.max(raw, axis=0, keepdims=True)))
             return tuple(higher)
 
@@ -591,7 +615,8 @@
         def weigh(tile, totals):
             sums = []
             for head in range(heads):
-                prob = jnp.exp2((scores[head, tile] - peaks[head]) * shift)
+                raw = scores[tile, :, head * rows : (head + 1) * rows]
+                prob = jnp.exp2((raw - peaks[head]) * shift)
                 sums.append(totals[head] + jnp.sum(prob, axis=0, keepdims=True))
                 at = slice(head * HEAD, (head + 1) * HEAD)
                 acc_t[at] += dot_nn(values_t[tile, at], prob.astype(BF16))
@@ -620,35 +645,30 @@
         def _():
             scatter1.send_far()
 
-            @when_swapped
-            def _():
-                wi_parts[0].pass_on(0)
-                wo_parts[0].bring()
-
         @pl.when(step == 2)
         def _():
             scatter1.send_near()
 
+        @pl.when((step == 2) & place.swapped)
+        def _():
+            wi_parts[0].pass_on(0)
+
         @pl.when((step == 3) & place.swapped)
         def _():
             wi_parts[1].pass_on(0)
-            wo_parts[1].bring()
 
         return carry
 
     lax.fori_loop(0, MEMBERS, attend, 0)
-
-    gather_dy.take_near()
-    gather_dy.take_far()
 
     @when_swapped
     def _():
-        for one in wi_parts:
-            one.pass_on(1)
-        for one in wo_parts:
-            one.pass_on(0)
-
-    scatter1.wait()
+        wi_parts[0].pass_on(1)
+        wi_parts[1].pass_on(1)
+        dy_trade.wait_recv()
+        gather_dy.start()
+
+    when_swapped(functools.partial(wo_parts[0].pass_on, 0))
     gain2 = gain_mlp[...]
 
     def add_resid(at):
@@ -657,16 +677,14 @@
         scale = lax.rsqrt(jnp.mean(total * total, axis=-1, keepdims=True) + EPSILON)
         normed_mlp[me, at] = (total * scale * gain2).astype(BF16)
 
-    each_rows(rows, 64, add_resid)
-    gather_n.start()
+    scatter1.finish(add_resid, gather_n.start)
+    gather_dy.take_near()
     gather_x.drain()
     scatter1.drain()
 
     @when_swapped
     def _():
-        for one in wo_parts:
-            one.pass_on(1)
-        for one in wi_parts + wo_parts:
+        for one in wi_parts:
             one.ready()
 
     @when_stays
@@ -674,85 +692,116 @@
         for one in wi_parts + wo_parts:
             one.local.wait()
 
-    gather_dy.take_corner()
-    scatter3 = Scatter(wire, place, part, near, joined, far_in)
-
-    def feed(step, carry):
+    scatter3 = Scatter(wire, place, part, near, joined, far_in, chunks)
+
+    def feed_order(step):
         flip_core = jnp.where((step == 1) | (step == 2), 1, 0)
         flip_chip = jnp.where(step >= 2, 1, 0)
-        block = place.member(flip_core, flip_chip)
+        return place.member(flip_core, flip_chip)
+
+    def feed(step, carry):
+        block = feed_order(step)
 
         @pl.when(step == 1)
         def _():
-            gather_n.take_near()
+            for number in range(chunks):
+                gather_n.take_near(number)
+
+        @pl.when((step == 1) & place.swapped)
+        def _():
+            wo_parts[1].pass_on(0)
+            wo_parts[0].pass_on(1)
 
         @pl.when(step == 2)
         def _():
-            gather_n.take_far()
-            gather_n.take_corner()
-
-        def units(number, inner):
-            at = pl.ds(pl.multiple_of(number * span, span), span)
-            hidden = dot_nn(normed_mlp[block], wi_m[:, at])
-            grad_active = dot_nt(dy_all[block], wo_m[at])
-            square = hidden * hidden
-            bend = jnp.tanh(GELU_A * hidden * (1.0 + GELU_B * square))
-            upper = 0.5 * (1.0 + bend)
-            active[block, :, at] = (hidden * upper).astype(BF16)
-            slope = upper + 0.5 * hidden * (1.0 - bend * bend) * (
-                GELU_A * (1.0 + 3.0 * GELU_B * square)
-            )
-            grad_hidden[block, :, at] = (grad_active * slope).astype(BF16)
-            return inner
-
-        lax.fori_loop(0, hidden_units // span, units, 0)
-
-        def across_features(number, inner):
-            at = pl.ds(pl.multiple_of(number * span, span), span)
-            part[block, :, at] = dot_nt(grad_hidden[block], wi_m[at]).astype(BF16)
-            outs[block, :, at] = dot_nn(active[block], wo_m[:, at]).astype(BF16)
-            return inner
-
-        lax.fori_loop(0, width // span, across_features, 0)
+            gather_dy.take_far()
+            for number in range(chunks):
+                gather_n.take_far(number)
+            for number in range(chunks):
+                gather_n.take_corner(number)
+
+        @pl.when((step == 2) & place.swapped)
+        def _():
+            wo_parts[1].pass_on(1)
+
+        hidden = dot_nn(normed_mlp[block], wi_m[...])
+        square = hidden * hidden
+        bend = jnp.tanh(GELU_A * hidden * (1.0 + GELU_B * square))
+        upper = 0.5 * (1.0 + bend)
+        active[block] = (hidden * upper).astype(BF16)
+        slopes[block] = upper + 0.5 * hidden * (1.0 - bend * bend) * (
+            GELU_A * (1.0 + 3.0 * GELU_B * square)
+        )
+        return carry
+
+    lax.fori_loop(0, MEMBERS, feed, 0)
+    gather_dy.take_corner()
+
+    @when_swapped
+    def _():
+        for one in wo_parts:
+            one.ready()
+
+    def feed_back(step, carry):
+        block = place.member(*swap_order(3 - step))
+
+        grad_active = dot_nt(dy_all[block], wo_m[...])
+        grad_hidden[block] = (grad_active * slopes[block]).astype(BF16)
+        part[block] = dot_nt(grad_hidden[block], wi_m[...]).astype(BF16)
+
+        @pl.when(step == 0)
+        def _():
+            scatter3.send_corner()
 
         @pl.when(step == 1)
         def _():
+            scatter3.send_far()
+
+        @pl.when(step == 2)
+        def _():
             scatter3.send_near()
 
-        @pl.when(step == 2)
-        def _():
-            scatter3.send_corner()
-
-        @pl.when(step == 3)
-        def _():
-            scatter3.send_far()
-
-        return carry
-
-    lax.fori_loop(0, MEMBERS, feed, 0)
+        return carry
+
+    lax.fori_loop(0, MEMBERS, feed_back, 0)
 
     ahead, back = tuple(range(bits)), tuple(reversed(range(bits)))
-    sum_in = Reduce(
-        wire, place, mlp_grads, 0, mlp_slots.at[pl.ds(0, width)],
-        mlp_sums.at[pl.ds(0, width)], ahead, local_sems.at[8],
-    )
-    sum_out = Reduce(
-        wire, place, mlp_grads, width, mlp_slots.at[pl.ds(width, hidden_units)],
-        mlp_sums.at[pl.ds(width, hidden_units)], back, local_sems.at[9],
-    )
-    split = 3 * width // 2
-    sum_one = Reduce(
-        wire, place, attn_grads, 0, attn_slots.at[pl.ds(0, split)],
-        attn_sums.at[pl.ds(0, split)], ahead, local_sems.at[10],
-    )
-    sum_two = Reduce(
-        wire, place, attn_grads, split, attn_slots.at[pl.ds(split, split)],
-        attn_sums.at[pl.ds(split, split)], back, local_sems.at[11],
-    )
-    sum_proj = Reduce(
-        wire, place, attn_grads, 3 * width, wa_slots,
-        attn_sums.at[pl.ds(3 * width, width)], ahead, local_sems.at[12],
-    )
+    used = [9]
+
+    def advance(*chains):
+        for chain in chains:
+            chain.advance()
+
+    def reduce(source, start, slots, slot_start, result, result_start, size, order):
+        used[0] += 1
+        return Reduce(
+            wire, place, source, start, slots.at[pl.ds(slot_start, size)],
+            result.at[pl.ds(result_start, size)], order, local_sems.at[used[0] - 1],
+        )
+
+    quarter = width // 2
+    sum_in = [
+        reduce(mlp_grads, n * quarter, mlp_slots, n * quarter, in_sums, n * quarter, quarter, ahead)
+        for n in range(2)
+    ]
+    quarter = hidden_units // 2
+    sum_out = [
+        reduce(
+            mlp_grads, width + n * quarter, mlp_slots, width + n * quarter,
+            out_sums, n * quarter, quarter, back,
+        )
+        for n in range(2)
+    ]
+    count = 4 if (3 * width // 4 >> bits) % 16 == 0 else 2
+    split = 3 * width // count
+    sum_qkv = [
+        reduce(
+            attn_grads, n * split, attn_slots, n * split, qkv_sums, n * split, split,
+            back if n % 2 else ahead,
+        )
+        for n in range(count)
+    ]
+    sum_proj = reduce(wa_grads, 0, wa_slots, 0, wa_sums, 0, wa_grads.shape[0], ahead)
 
     def in_grads(number, carry):
         at = pl.ds(pl.multiple_of(number * span, span), span)
@@ -769,13 +818,24 @@
         mlp_grads[down] = dot_tn(left, right).astype(BF16)
         return carry
 
-    lax.fori_loop(0, width // span, in_grads, 0)
-    sum_in.advance()
-    lax.fori_loop(0, hidden_units // span, out_grads, 0)
-    sum_out.advance()
-
-    scatter3.wait()
+    for n in range(2):
+        count = width // span // 2
+        lax.fori_loop(n * count, (n + 1) * count, in_grads, 0)
+        sum_in[n].advance()
+        count = hidden_units // span // 2
+        lax.fori_loop(n * count, (n + 1) * count, out_grads, 0)
+        sum_out[n].advance()
+
+    def feed_out(block, carry):
+        outs[block] = dot_nn(active[block], wo_m[...]).astype(BF16)
+        return carry
+
+    lax.fori_loop(0, MEMBERS, feed_out, 0)
+    scatter2 = Scatter(wire, place, outs, near2, joined2, far2)
+    scatter2.send_corner()
+    scatter2.send_near()
     gain_sum[...] = jnp.zeros_like(gain_sum)
+    scores[...] = jnp.zeros_like(scores)
 
     def norm_back(at):
         grad = scatter3.total(at)
@@ -790,31 +850,31 @@
         grad_resid[at] = total
         grad_all[me, at] = total.astype(BF16)
 
-    each_rows(rows, 64, norm_back)
-    gather_g.start()
+    scatter3.finish(norm_back, gather_g.start)
     scatter3.drain()
-    scatter2 = Scatter(wire, place, outs, near2, joined2, far2)
-    scatter2.send_corner()
-    scatter2.send_near()
-    scores[...] = jnp.zeros_like(scores)
+    scatter2.send_far()
 
     def block_back(step, carry):
         block = place.member(*swap_order(step))
 
         @pl.when(step == 1)
         def _():
-            gather_g.take_near()
+            for number in range(chunks):
+                gather_g.take_near(number)
+            sum_in[0].advance()
+            sum_out[0].advance()
 
         @pl.when(step == 2)
         def _():
-            gather_g.take_far()
-            scatter2.send_far()
-            sum_in.advance()
+            advance(sum_in[0], sum_out[0])
+            for number in range(chunks):
+                gather_g.take_far(number)
+            advance(sum_in[1], sum_out[1])
 
         @pl.when(step == 3)
         def _():
-            sum_out.advance()
-            gather_g.take_corner()
+            for number in range(chunks):
+                gather_g.take_corner(number)
 
         source = grad_all[block]
         top = dot_nt(source, wa_m[...]).astype(BF16)
@@ -838,8 +898,10 @@
                 )
                 grad_prob = dot_nt(qkv[2, head, tile], tops[head])
                 grad_score = (prob * (grad_prob - deltas[head])).astype(BF16)
-                scores[head, tile, :, 128 : 128 + HEAD] += dot_nn(prob.astype(BF16), tops[head])
-                scores[head, tile, :, 0:HEAD] += dot_nn(grad_score, query)
+                scores[tile, :, head * 256 + 128 : head * 256 + 128 + HEAD] += dot_nn(
+                    prob.astype(BF16), tops[head]
+                )
+                scores[tile, :, head * 256 : head * 256 + HEAD] += dot_nn(grad_score, query)
                 acc_t[at] += dot_nn(keys_t[tile, at], grad_score)
             return inner
 
@@ -852,41 +914,42 @@
     def settle_heads(block, carry):
         for head in range(heads):
             at = slice(head * HEAD, (head + 1) * HEAD)
-            grad_keys = scores[head, block, :, 0:HEAD] * scaling
+            grad_keys = scores[block, :, head * 256 : head * 256 + HEAD] * scaling
             projected[1, block, :, at] = grad_keys.astype(BF16)
-            projected[2, block, :, at] = scores[head, block, :, 128 : 128 + HEAD].astype(BF16)
+            grad_values = scores[block, :, head * 256 + 128 : head * 256 + 128 + HEAD]
+            projected[2, block, :, at] = grad_values.astype(BF16)
         return carry
 
     lax.fori_loop(0, MEMBERS, settle_heads, 0)
 
+    def finish_output(at):
+        out_keep[at] = (resid[at] + scatter2.total(at)).astype(BF16)
+
+    scatter2.finish(finish_output)
+    out_trade = wire.copy(out_keep, out_in, place.trade())
+    when_swapped(out_trade.start)
+    advance(sum_in[1], sum_out[1])
+
+    def qkv_grads(kind, carry):
+        to = pl.ds(pl.multiple_of(kind * width, width), width)
+        left = normed[...].reshape(frame_count, width)
+        right = projected[kind].reshape(frame_count, features)
+        attn_grads[to] = dot_tn(left, right).astype(BF16)
+        return carry
+
     for kind in range(3):
-
-        def qkv_grads(number, carry, kind=kind):
-            at = pl.ds(pl.multiple_of(number * span, span), span)
-            to = pl.ds(pl.multiple_of(kind * width + number * span, span), span)
-            left = normed[:, :, at].reshape(frame_count, span)
-            right = projected[kind].reshape(frame_count, features)
-            attn_grads[to] = dot_tn(left, right).astype(BF16)
-            return carry
-
-        lax.fori_loop(0, width // span, qkv_grads, 0)
-
-    sum_one.advance()
-    sum_two.advance()
-    scatter4 = Scatter(wire, place, part, near, joined, far_in)
+        lax.fori_loop(kind, kind + 1, qkv_grads, 0)
+        done = (kind + 1) * count // 3
+        advance(*sum_qkv[kind * count // 3 : done])
+    scatter4 = Scatter(wire, place, part, near, joined, far_in, chunks)
 
     def inputs_back(step, carry):
         block = place.member(*swap_order(3 - step))
 
-        def columns(number, inner):
-            down = pl.ds(pl.multiple_of(number * span, span), span)
-            total = dot_nt(projected[0, block], wq_m[0, down])
-            total += dot_nt(projected[1, block], wq_m[1, down])
-            total += dot_nt(projected[2, block], wq_m[2, down])
-            part[block, :, down] = total.astype(BF16)
-            return inner
-
-        lax.fori_loop(0, width // span, columns, 0)
+        total = dot_nt(projected[0, block], wq_m[0])
+        total += dot_nt(projected[1, block], wq_m[1])
+        total += dot_nt(projected[2, block], wq_m[2])
+        part[block] = total.astype(BF16)
 
         @pl.when(step == 0)
         def _():
@@ -904,32 +967,31 @@
 
     lax.fori_loop(0, MEMBERS, inputs_back, 0)
 
-    def proj_grads(number, carry):
-        at = pl.ds(pl.multiple_of(number * features, features), features)
-        to = pl.ds(pl.multiple_of(3 * width + number * features, features), features)
-        total = dot_nn(att_t[0], grad_all[0, :, at])
-        for member in range(1, MEMBERS):
-            total += dot_nn(att_t[member], grad_all[member, :, at])
-        attn_grads[to] = total.astype(BF16)
-        return carry
-
-    lax.fori_loop(0, width // features, proj_grads, 0)
-    sum_proj.advance()
-    sum_in.advance()
-    scatter2.wait()
-
-    def finish_output(at):
-        out_keep[at] = (resid[at] + scatter2.total(at)).astype(BF16)
-
-    each_rows(rows, 64, finish_output)
-    out_trade = wire.copy(out_keep, out_in, place.trade())
-    when_swapped(out_trade.start)
-    sum_out.advance()
-    sum_one.advance()
-    sum_two.advance()
-    sum_proj.advance()
-
-    scatter4.wait()
+    if wa_grads.shape[1] == width:
+        blocks = [att_t[member] for member in range(MEMBERS)]
+
+        def proj_grads(number, carry):
+            at = pl.ds(pl.multiple_of(number * span, span), span)
+            total = dot_nn(blocks[0], grad_all[0, :, at])
+            for member in range(1, MEMBERS):
+                total += dot_nn(blocks[member], grad_all[member, :, at])
+            wa_grads[:, at] = total.astype(BF16)
+            return carry
+
+        lax.fori_loop(0, width // span, proj_grads, 0)
+    else:
+
+        def proj_grads(number, carry):
+            at = pl.ds(pl.multiple_of(number * features, features), features)
+            total = dot_nn(att_t[0], grad_all[0, :, at])
+            for member in range(1, MEMBERS):
+                total += dot_nn(att_t[member], grad_all[member, :, at])
+            wa_grads[at] = total.astype(BF16)
+            return carry
+
+        lax.fori_loop(0, width // features, proj_grads, 0)
+    advance(sum_proj, sum_in[0], sum_out[0])
+    advance(*sum_qkv[:2], sum_proj, *sum_qkv[2:], sum_in[0], sum_out[0])
 
     def finish_frames(at):
         grad = scatter4.total(at)
@@ -942,9 +1004,12 @@
         grad_frames[at] = total
         moved[at] = total.astype(BF16)
 
-    each_rows(rows, 64, finish_frames)
-    frames_trade = wire.copy(moved, moved_in, place.trade())
-    when_swapped(frames_trade.start)
+    frames_trades = []
+    for number in range(chunks):
+        at = pl.ds(number * half, half)
+        frames_trades.append(wire.copy(moved.at[at], moved_in.at[at], place.trade()))
+
+    scatter4.finish(finish_frames, lambda number: when_swapped(frames_trades[number].start))
 
     partners = [place.sibling(), place.across(), {"pair": 1 - place.pair}]
     partners += [place.column(bit) for bit in range(bits)]
@@ -962,7 +1027,11 @@
 
     gain_trades[0].start()
     gain_chain = Steps([functools.partial(gain_step, n) for n in range(len(partners))])
-    sums = [sum_one, sum_two, sum_proj, sum_in, sum_out]
+    sums = sum_qkv + [sum_proj] + sum_in + sum_out
+    early, late = sum_qkv[:2], sum_qkv[2:]
+    advance(*early, sum_proj, sum_in[1], sum_out[1], *late, sum_in[0], sum_out[0], gain_chain)
+    advance(sum_in[1], sum_out[1], *early, gain_chain, sum_proj, *late, gain_chain)
+    advance(sum_in[1], sum_out[1], *early, sum_proj, *late, gain_chain)
     advance_all([gain_chain] + sums)
     gains_out[...] = gain_sum[8 * len(partners) : 8 * len(partners) + 8]
 
@@ -970,11 +1039,10 @@
     def _():
         out_trade.wait_recv()
         output[...] = out_in[...]
-        frames_trade.wait_recv()
+        for one in frames_trades:
+            one.wait_recv()
         grad_frames[...] = moved_in[...].astype(F32)
-        out_trade.wait_send()
-        frames_trade.wait_send()
-        for one in x_trades + [dy_trade]:
+        for one in x_trades + frames_trades + [dy_trade, out_trade]:
             one.wait_send()
         for one in weights:
             one.drain()
@@ -1000,13 +1068,16 @@
     frames = MEMBERS * rows
     steps = 3 + bits
     members = (MEMBERS, rows, width)
+    wa_shape = wa.shape if (features >> bits) % 16 == 0 else (width, features)
     block = pl.BlockSpec(memory_space=pltpu.VMEM)
     whole = pl.BlockSpec(memory_space=pl.ANY)
     outputs = [
         ((rows, width), BF16, block),
         ((rows, width), F32, block),
-        ((width + units, width), BF16, whole),
-        ((4 * width, features), BF16, whole),
+        ((width, units), BF16, whole),
+        ((units, width), BF16, whole),
+        ((3 * width, features), BF16, whole),
+        (wa_shape, BF16, whole),
         ((8, width), F32, block),
     ]
     scratch = [
@@ -1029,7 +1100,7 @@
         ((MEMBERS, 8, rows), F32),
         ((8, frames), jnp.int32),
         ((2, 8, frames), jnp.int32),
-        ((heads, MEMBERS, rows, rows), F32),
+        ((MEMBERS, rows, max(heads * max(rows, 256), units)), F32),
     ]
     scatter = [(members, BF16), ((2, rows, width), BF16), ((rows, width), BF16),
                ((rows, width), BF16)]
@@ -1039,15 +1110,16 @@
         ((rows, width), F32),
         ((width + units, width), BF16),
         ((width + units, width), BF16),
-        ((4 * width, features), BF16),
         ((3 * width, features), BF16),
-        ((width, features), BF16),
+        ((3 * width, features), BF16),
+        (wa_shape, BF16),
+        (wa_shape, BF16),
         ((3, MEMBERS, rows, features), BF16),
         ((8 * steps + 8, width), F32),
         ((steps, 8, width), F32),
     ]
     scratch += [((rows, width), BF16)] * 4
-    count = 64 + 5 * (3 * bits + 2)
+    count = 72 + 9 * (3 * bits + 2)
     return pl.pallas_call(
         functools.partial(layer_kernel, lengths.shape[1], bits),
         out_shape=[jax.ShapeDtypeStruct(shape, kind) for shape, kind, _ in outputs],
@@ -1058,7 +1130,7 @@
         + [
             pltpu.SemaphoreType.DMA((count,)),
             pltpu.SemaphoreType.DMA((count,)),
-            pltpu.SemaphoreType.DMA((13,)),
+            pltpu.SemaphoreType.DMA((20,)),
         ],
         compiler_params=pltpu.CompilerParams(
             collective_id=0, has_side_effects=True, vmem_limit_bytes=VMEM_LIMIT
@@ -1070,22 +1142,20 @@
 def per_device(bits, frames, lengths, wq, wa, wi, wo, gain_attn, gain_mlp, cotangent):
     width = frames.shape[1]
     features = wa.shape[0]
-    output, grad_frames, mlp_sums, attn_sums, gains = layer_call(
+    output, grad_frames, in_sums, out_sums, qkv_sums, wa_sums, gains = layer_call(
         bits, frames, cotangent, lengths, gain_attn.reshape(1, width),
         gain_mlp.reshape(1, width), wq, wa, wi, wo,
     )
-    mlp_sums = mlp_sums.astype(F32)
-    attn_sums = attn_sums.astype(F32)
-    grad_wq = attn_sums[: 3 * width].reshape(3, width, features)
-    turned = attn_sums[3 * width :].reshape(width // features, features, features)
-    grad_wa = jnp.transpose(turned, (1, 0, 2)).reshape(features, width)
+    if wa_sums.shape != wa.shape:
+        turned = wa_sums.reshape(width // features, features, features)
+        wa_sums = jnp.transpose(turned, (1, 0, 2)).reshape(features, width)
     return (
         output,
         grad_frames,
-        grad_wq,
-        grad_wa,
-        mlp_sums[:width],
-        mlp_sums[width:],
+        qkv_sums.astype(F32).reshape(3, width, features),
+        wa_sums.astype(F32),
+        in_sums.astype(F32),
+        out_sums.astype(F32),
         gains[1],
         gains[0],
     )

time: 267 us -> 230 us (0.86)
  Pallas kernels: 253 us -> 216 us
  local copies, waits for them, and re-layouts: 13.1 us -> 3.22 us
  other arithmetic: 0 us -> 9.71 us
    pallas_call x1, Pallas kernels: 253 us -> 216 us  [layer_call(): pl.pallas_call(functools.partial(layer_kernel, lengths.shape[1], bits), o...]
    slice x3 -> x0, local copies, waits for them, and re-layouts: 8.79 us -> none  [the longest x1 6.81 us: per_device(): mlp_sums[width:]]
    convert_element_type x0 -> x3, other arithmetic: none -> 7.78 us  [the longest x1 4.22 us: per_device(): in_sums.astype(F32)]
where the time goes in v4:
time: 230 us
  Pallas kernels  216 us (94%)
  other arithmetic  9.71 us (4%)
  local copies, waits for them, and re-layouts  3.22 us (1%)
    pallas_call x1, Pallas kernels, layer_call(): pl.pallas_call(functools.partial(layer_kernel, lengths.shape[1], bits), o...  216 us

profile of v4, /device:TPU:0, one launch (start us, length us, event | category | flops | bytes accessed | tf_op | source)
XLA Modules:
  0.0 230.0 jit_solution(17526442361080339001)
XLA Ops:
  0.6 216.5 %layer.1 = (bf16[256,1024]{1,0:T(8,128)(2,1)}, f32[256,1024]{1,0:T(8,128)}, bf16[1024,1024]{1,0:T(8,128)(2,1)}, bf16[1024,1024]{1,0:T(8,128)(2,1)}, bf16[3072,25...) custom-call(bf16[256,1024]{1,0:T(8,128)(2,1)} %x_own.1, bf16[256,1024]{1,0:T(8,128)(2,1)} %dy_own.1, ...), custom_call_target="tpu_custom_call" | custom-call | tf_op jit(solution)/shard_map/layer/pallas_call | solution.py:1123
  217.1 1.4 fusion
  218.5 0.0 copy-start
  218.5 4.2 %convert_element_type.11 = f32[1024,1024]{1,0:T(8,128)} convert(bf16[1024,1024]{1,0:T(8,128)(2,1)} %get-tuple-element.19) | non-fusion elementwise | flops 1048576 | bytes 6291456 | tf_op jit(solution)/shard_map/convert_element_type | solution.py:1157
  222.8 0.0 copy-done
  222.8 0.0 copy-start.1
  222.8 2.5 %convert_element_type.12 = f32[1024,1024]{1,0:T(8,128)} convert(bf16[1024,1024]{1,0:T(8,128)(2,1)S(1)} %copy-done) | non-fusion elementwise | flops 1048576 | bytes 6291456 | tf_op jit(solution)/shard_map/convert_element_type | solution.py:1158
  225.2 0.0 copy-done.1
  225.2 0.0 copy-start.3
  225.2 0.0 copy-start.4
  225.2 1.9 convert.1
  227.2 0.0 copy-start.2
  227.2 0.0 copy-done.3
  227.2 1.1 convert_element_type.10
  228.3 0.0 copy-done.4
  228.3 0.8 copy.19
  229.1 0.0 copy-done.2
  229.1 1.0 copy.20
Async XLA Ops:
  218.5 4.2 %copy-start = (bf16[1024,1024]{1,0:T(8,128)(2,1)S(1)}, bf16[1024,1024]{1,0:T(8,128)(2,1)}, u32[]{:S(2)}) copy-start(bf16[1024,1024]{1,0:T(8,128)(2,1)} %get-tuple-element.20) | copy-start | bytes 6291460
  222.8 2.5 %copy-start.1 = (bf16[3072,256]{1,0:T(8,128)(2,1)S(1)}, bf16[3072,256]{1,0:T(8,128)(2,1)}, u32[]{:S(2)}) copy-start(bf16[3072,256]{1,0:T(8,128)(2,1)} %get-tuple-element.17) | copy-start | bytes 4718596
  225.2 1.9 copy-start.3
  225.2 3.0 %copy-start.4 = (bf16[256,1024]{1,0:T(8,128)(2,1)S(1)}, bf16[256,1024]{1,0:T(8,128)(2,1)}, u32[]{:S(2)}) copy-start(bf16[256,1024]{1,0:T(8,128)(2,1)} %get-tuple-element.32) | copy-start | bytes 1572868
  227.2 1.9 copy-start.2

commit v5 on v4

--- a/solution.py
+++ b/solution.py
@@ -65,6 +65,10 @@
         step = 1 << bit
         here = lax.rem(lax.div(self.col, step), 2)
         return {"col": self.col + step * (1 - 2 * here)}
+
+    def columns(self):
+        first, second = self.column(0)["col"], self.column(1)["col"]
+        return [{"col": first + second - self.col}, {"col": first}, {"col": second}]
 
 
 class Wire:
@@ -342,40 +346,36 @@
 
 
 class Weight:
-    def __init__(self, wire, place, source, target, axis, start, size, order, local_sem):
+    def __init__(self, wire, place, source, target, axis, start, size, local_sem):
         quarter = lax.rem(place.col, MEMBERS)
-        if order[0] == 1:
-            quarter = 2 * lax.rem(quarter, 2) + lax.div(quarter, 2)
         depth = size // MEMBERS
 
         def cut(ref, first, many):
             at = window(start + first, many)
             return ref.at[:, at] if axis == 1 else ref.at[at]
 
-        other = quarter + 1 - 2 * lax.rem(quarter, 2)
-        duo = lax.div(quarter, 2)
         mine = cut(target, quarter * depth, depth)
-        both = cut(target, duo * 2 * depth, 2 * depth)
-        rest = cut(target, (1 - duo) * 2 * depth, 2 * depth)
-        self.moves = [
-            wire.copy(cut(source, quarter * depth, depth), mine, place.trade()),
-            wire.copy(mine, mine, place.column(order[0]), cut(target, other * depth, depth)),
-            wire.copy(both, both, place.column(order[1]), rest),
-        ]
+        self.cross = wire.copy(cut(source, quarter * depth, depth), mine, place.trade())
+        self.spread = []
+        for other in place.columns():
+            theirs = cut(target, lax.rem(other["col"], MEMBERS) * depth, depth)
+            self.spread.append(wire.copy(mine, mine, other, theirs))
         self.local = pltpu.make_async_copy(cut(source, 0, size), cut(target, 0, size), local_sem)
 
     def bring(self):
-        self.moves[0].start()
-
-    def pass_on(self, step):
-        self.moves[step].wait_recv()
-        self.moves[step + 1].start()
+        self.cross.start()
+
+    def pass_on(self):
+        self.cross.wait_recv()
+        for one in self.spread:
+            one.start()
 
     def ready(self):
-        self.moves[2].wait_recv()
+        for one in self.spread:
+            one.wait_recv()
 
     def drain(self):
-        for one in self.moves:
+        for one in [self.cross] + self.spread:
             one.wait_send()
 
 
@@ -444,26 +444,25 @@
     x_local = pltpu.make_async_copy(x_own, x_all.at[me], local_sems.at[0])
     dy_local = pltpu.make_async_copy(dy_own, dy_all.at[me], local_sems.at[1])
 
-    def weight(number, source, target, axis, start, size, order):
-        return Weight(
-            wire, place, source, target, axis, start, size, order, local_sems.at[2 + number]
-        )
+    def weight(number, source, target, axis, start, size):
+        return Weight(wire, place, source, target, axis, start, size, local_sems.at[2 + number])
 
     def halves(number, source, target, axis):
         size = source.shape[axis] // 2
         return [
-            weight(number + n, source, target, axis, n * size, size, (n, 1 - n)) for n in range(2)
+            weight(number + n, source, target, axis, n * size, size) for n in range(2)
         ]
 
     wq_parts = halves(0, wq, wq_m, 1)
     wi_parts = halves(2, wi, wi_m, 0)
     wo_parts = halves(4, wo, wo_m, 0)
-    wa_part = weight(6, wa, wa_m, 0, 0, features, (1, 0))
+    wa_part = weight(6, wa, wa_m, 0, 0, features)
     weights = wq_parts + [wa_part] + wi_parts + wo_parts
 
     meet(
         [place.sibling(), place.across(), place.trade(), {"pair": 1 - place.pair}]
-        + [place.column(bit) for bit in range(bits)]
+        + place.columns()
+        + [place.column(bit) for bit in range(2, bits)]
     )
 
     @when_swapped
@@ -501,9 +500,7 @@
     @when_swapped
     def _():
         for one in wq_parts:
-            one.pass_on(0)
-        for one in wq_parts:
-            one.pass_on(1)
+            one.pass_on()
         for number in range(chunks):
             x_trades[number].wait_recv()
             gather_x.start(number)
@@ -574,7 +571,7 @@
 
         @pl.when((step == 2) & place.swapped)
         def _():
-            wa_part.pass_on(0)
+            wa_part.pass_on()
 
         project(member)
         return carry
@@ -586,7 +583,6 @@
     @when_swapped
     def _():
         first[...] = first_near[1]
-        wa_part.pass_on(1)
 
     @when_stays
     def _():
@@ -649,26 +645,17 @@
         def _():
             scatter1.send_near()
 
-        @pl.when((step == 2) & place.swapped)
-        def _():
-            wi_parts[0].pass_on(0)
-
-        @pl.when((step == 3) & place.swapped)
-        def _():
-            wi_parts[1].pass_on(0)
-
         return carry
 
     lax.fori_loop(0, MEMBERS, attend, 0)
 
     @when_swapped
     def _():
-        wi_parts[0].pass_on(1)
-        wi_parts[1].pass_on(1)
+        wi_parts[0].pass_on()
+        wi_parts[1].pass_on()
         dy_trade.wait_recv()
         gather_dy.start()
 
-    when_swapped(functools.partial(wo_parts[0].pass_on, 0))
     gain2 = gain_mlp[...]
 
     def add_resid(at):
@@ -709,8 +696,7 @@
 
         @pl.when((step == 1) & place.swapped)
         def _():
-            wo_parts[1].pass_on(0)
-            wo_parts[0].pass_on(1)
+            wo_parts[0].pass_on()
 
         @pl.when(step == 2)
         def _():
@@ -722,7 +708,7 @@
 
         @pl.when((step == 2) & place.swapped)
         def _():
-            wo_parts[1].pass_on(1)
+            wo_parts[1].pass_on()
 
         hidden = dot_nn(normed_mlp[block], wi_m[...])
         square = hidden * hidden
@@ -736,35 +722,6 @@
 
     lax.fori_loop(0, MEMBERS, feed, 0)
     gather_dy.take_corner()
-
-    @when_swapped
-    def _():
-        for one in wo_parts:
-            one.ready()
-
-    def feed_back(step, carry):
-        block = place.member(*swap_order(3 - step))
-
-        grad_active = dot_nt(dy_all[block], wo_m[...])
-        grad_hidden[block] = (grad_active * slopes[block]).astype(BF16)
-        part[block] = dot_nt(grad_hidden[block], wi_m[...]).astype(BF16)
-
-        @pl.when(step == 0)
-        def _():
-            scatter3.send_corner()
-
-        @pl.when(step == 1)
-        def _():
-            scatter3.send_far()
-
-        @pl.when(step == 2)
-        def _():
-            scatter3.send_near()
-
-        return carry
-
-    lax.fori_loop(0, MEMBERS, feed_back, 0)
-
     ahead, back = tuple(range(bits)), tuple(reversed(range(bits)))
     used = [9]
 
@@ -780,17 +737,19 @@
         )
 
     quarter = width // 2
+    half_in, half_out = width // 2, hidden_units // 2
     sum_in = [
-        reduce(mlp_grads, n * quarter, mlp_slots, n * quarter, in_sums, n * quarter, quarter, ahead)
-        for n in range(2)
+        reduce(
+            mlp_grads, n * half_in, mlp_slots, n * half_in, in_sums, n * half_in, half_in, order
+        )
+        for n, order in enumerate((ahead, back))
     ]
-    quarter = hidden_units // 2
     sum_out = [
         reduce(
-            mlp_grads, width + n * quarter, mlp_slots, width + n * quarter,
-            out_sums, n * quarter, quarter, back,
+            mlp_grads, width + n * half_out, mlp_slots, width + n * half_out,
+            out_sums, n * half_out, half_out, order,
         )
-        for n in range(2)
+        for n, order in enumerate((ahead, back))
     ]
     count = 4 if (3 * width // 4 >> bits) % 16 == 0 else 2
     split = 3 * width // count
@@ -818,19 +777,50 @@
         mlp_grads[down] = dot_tn(left, right).astype(BF16)
         return carry
 
+    tiles_here = hidden_units // span // 2
     for n in range(2):
-        count = width // span // 2
-        lax.fori_loop(n * count, (n + 1) * count, in_grads, 0)
+        lax.fori_loop(n * tiles_here, (n + 1) * tiles_here, out_grads, 0)
+        sum_out[n].advance()
+
+    @when_swapped
+    def _():
+        for one in wo_parts:
+            one.ready()
+
+    def feed_back(step, carry):
+        block = place.member(*swap_order(3 - step))
+
+        grad_active = dot_nt(dy_all[block], wo_m[...])
+        grad_hidden[block] = (grad_active * slopes[block]).astype(BF16)
+        part[block] = dot_nt(grad_hidden[block], wi_m[...]).astype(BF16)
+
+        @pl.when(step == 0)
+        def _():
+            scatter3.send_corner()
+
+        @pl.when(step == 1)
+        def _():
+            scatter3.send_far()
+
+        @pl.when(step == 2)
+        def _():
+            scatter3.send_near()
+
+        return carry
+
+    lax.fori_loop(0, MEMBERS, feed_back, 0)
+
+    tiles_here = width // span // 2
+    for n in range(2):
+        lax.fori_loop(n * tiles_here, (n + 1) * tiles_here, in_grads, 0)
         sum_in[n].advance()
-        count = hidden_units // span // 2
-        lax.fori_loop(n * count, (n + 1) * count, out_grads, 0)
-        sum_out[n].advance()
 
     def feed_out(block, carry):
         outs[block] = dot_nn(active[block], wo_m[...]).astype(BF16)
         return carry
 
     lax.fori_loop(0, MEMBERS, feed_out, 0)
+    advance(*sum_out)
     scatter2 = Scatter(wire, place, outs, near2, joined2, far2)
     scatter2.send_corner()
     scatter2.send_near()
@@ -853,6 +843,7 @@
     scatter3.finish(norm_back, gather_g.start)
     scatter3.drain()
     scatter2.send_far()
+    advance(*sum_out)
 
     def block_back(step, carry):
         block = place.member(*swap_order(step))
@@ -861,20 +852,18 @@
         def _():
             for number in range(chunks):
                 gather_g.take_near(number)
-            sum_in[0].advance()
-            sum_out[0].advance()
+            advance(*sum_in)
 
         @pl.when(step == 2)
         def _():
-            advance(sum_in[0], sum_out[0])
             for number in range(chunks):
                 gather_g.take_far(number)
-            advance(sum_in[1], sum_out[1])
 
         @pl.when(step == 3)
         def _():
             for number in range(chunks):
                 gather_g.take_corner(number)
+            advance(*sum_in)
 
         source = grad_all[block]
         top = dot_nt(source, wa_m[...]).astype(BF16)
@@ -911,6 +900,31 @@
 
     lax.fori_loop(0, MEMBERS, block_back, 0)
 
+    if wa_grads.shape[1] == width:
+        blocks = [att_t[member] for member in range(MEMBERS)]
+
+        def proj_grads(number, carry):
+            at = pl.ds(pl.multiple_of(number * span, span), span)
+            total = dot_nn(blocks[0], grad_all[0, :, at])
+            for member in range(1, MEMBERS):
+                total += dot_nn(blocks[member], grad_all[member, :, at])
+            wa_grads[:, at] = total.astype(BF16)
+            return carry
+
+        lax.fori_loop(0, width // span, proj_grads, 0)
+    else:
+
+        def proj_grads(number, carry):
+            at = pl.ds(pl.multiple_of(number * features, features), features)
+            total = dot_nn(att_t[0], grad_all[0, :, at])
+            for member in range(1, MEMBERS):
+                total += dot_nn(att_t[member], grad_all[member, :, at])
+            wa_grads[at] = total.astype(BF16)
+            return carry
+
+        lax.fori_loop(0, width // features, proj_grads, 0)
+    advance(sum_proj)
+
     def settle_heads(block, carry):
         for head in range(heads):
             at = slice(head * HEAD, (head + 1) * HEAD)
@@ -925,10 +939,7 @@
     def finish_output(at):
         out_keep[at] = (resid[at] + scatter2.total(at)).astype(BF16)
 
-    scatter2.finish(finish_output)
-    out_trade = wire.copy(out_keep, out_in, place.trade())
-    when_swapped(out_trade.start)
-    advance(sum_in[1], sum_out[1])
+    advance(*sum_out)
 
     def qkv_grads(kind, carry):
         to = pl.ds(pl.multiple_of(kind * width, width), width)
@@ -967,31 +978,11 @@
 
     lax.fori_loop(0, MEMBERS, inputs_back, 0)
 
-    if wa_grads.shape[1] == width:
-        blocks = [att_t[member] for member in range(MEMBERS)]
-
-        def proj_grads(number, carry):
-            at = pl.ds(pl.multiple_of(number * span, span), span)
-            total = dot_nn(blocks[0], grad_all[0, :, at])
-            for member in range(1, MEMBERS):
-                total += dot_nn(blocks[member], grad_all[member, :, at])
-            wa_grads[:, at] = total.astype(BF16)
-            return carry
-
-        lax.fori_loop(0, width // span, proj_grads, 0)
-    else:
-
-        def proj_grads(number, carry):
-            at = pl.ds(pl.multiple_of(number * features, features), features)
-            total = dot_nn(att_t[0], grad_all[0, :, at])
-            for member in range(1, MEMBERS):
-                total += dot_nn(att_t[member], grad_all[member, :, at])
-            wa_grads[at] = total.astype(BF16)
-            return carry
-
-        lax.fori_loop(0, width // features, proj_grads, 0)
-    advance(sum_proj, sum_in[0], sum_out[0])
-    advance(*sum_qkv[:2], sum_proj, *sum_qkv[2:], sum_in[0], sum_out[0])
+    scatter2.finish(finish_output)
+    out_trade = wire.copy(out_keep, out_in, place.trade())
+    when_swapped(out_trade.start)
+    advance(sum_proj, *sum_out)
+    advance(*sum_qkv[:2], *sum_qkv[2:], *sum_in)
 
     def finish_frames(at):
         grad = scatter4.total(at)
@@ -1029,9 +1020,9 @@
     gain_chain = Steps([functools.partial(gain_step, n) for n in range(len(partners))])
     sums = sum_qkv + [sum_proj] + sum_in + sum_out
     early, late = sum_qkv[:2], sum_qkv[2:]
-    advance(*early, sum_proj, sum_in[1], sum_out[1], *late, sum_in[0], sum_out[0], gain_chain)
-    advance(sum_in[1], sum_out[1], *early, gain_chain, sum_proj, *late, gain_chain)
-    advance(sum_in[1], sum_out[1], *early, sum_proj, *late, gain_chain)
+    advance(*early, sum_proj, *sum_out, *late, *sum_in, gain_chain)
+    advance(*early, gain_chain, sum_proj, *late, gain_chain, *sum_in)
+    advance(*early, sum_proj, *late, gain_chain)
     advance_all([gain_chain] + sums)
     gains_out[...] = gain_sum[8 * len(partners) : 8 * len(partners) + 8]
 
@@ -1119,7 +1110,7 @@
         ((steps, 8, width), F32),
     ]
     scratch += [((rows, width), BF16)] * 4
-    count = 72 + 9 * (3 * bits + 2)
+    count = 120 + 9 * (3 * bits + 2)
     return pl.pallas_call(
         functools.partial(layer_kernel, lengths.shape[1], bits),
         out_shape=[jax.ShapeDtypeStruct(shape, kind) for shape, kind, _ in outputs],

time: 230 us -> 222 us (0.965)
  Pallas kernels: 216 us -> 208 us
    pallas_call x1, Pallas kernels: 216 us -> 208 us  [layer_call(): pl.pallas_call(functools.partial(layer_kernel, lengths.shape[1], bits), o...]
where the time goes in v5:
time: 222 us
  Pallas kernels  208 us (94%)
  other arithmetic  9.71 us (4%)
  local copies, waits for them, and re-layouts  3.22 us (1%)
    pallas_call x1, Pallas kernels, layer_call(): pl.pallas_call(functools.partial(layer_kernel, lengths.shape[1], bits), o...  208 us

profile of v5, /device:TPU:0, one launch (start us, length us, event | category | flops | bytes accessed | tf_op | source)
XLA Modules:
  0.0 221.7 jit_solution(4969635110012540112)
XLA Ops:
  0.6 208.2 %layer.1 = (bf16[256,1024]{1,0:T(8,128)(2,1)}, f32[256,1024]{1,0:T(8,128)}, bf16[1024,1024]{1,0:T(8,128)(2,1)}, bf16[1024,1024]{1,0:T(8,128)(2,1)}, bf16[3072,25...) custom-call(bf16[256,1024]{1,0:T(8,128)(2,1)} %x_own.1, bf16[256,1024]{1,0:T(8,128)(2,1)} %dy_own.1, ...), custom_call_target="tpu_custom_call" | custom-call | tf_op jit(solution)/shard_map/layer/pallas_call | solution.py:1114
  208.8 1.4 fusion
  210.2 0.0 copy-start
  210.2 4.2 %convert_element_type.11 = f32[1024,1024]{1,0:T(8,128)} convert(bf16[1024,1024]{1,0:T(8,128)(2,1)} %get-tuple-element.19) | non-fusion elementwise | flops 1048576 | bytes 6291456 | tf_op jit(solution)/shard_map/convert_element_type | solution.py:1148
  214.5 0.0 copy-done
  214.5 0.0 copy-start.1
  214.5 2.5 %convert_element_type.12 = f32[1024,1024]{1,0:T(8,128)} convert(bf16[1024,1024]{1,0:T(8,128)(2,1)S(1)} %copy-done) | non-fusion elementwise | flops 1048576 | bytes 6291456 | tf_op jit(solution)/shard_map/convert_element_type | solution.py:1149
  216.9 0.0 copy-done.1
  216.9 0.0 copy-start.3
  216.9 0.0 copy-start.4
  216.9 1.9 convert.1
  218.9 0.0 copy-start.2
  218.9 0.0 copy-done.3
  218.9 1.1 convert_element_type.10
  220.0 0.0 copy-done.4
  220.0 0.8 copy.19
  220.8 0.0 copy-done.2
  220.8 1.0 copy.20
Async XLA Ops:
  210.2 4.2 %copy-start = (bf16[1024,1024]{1,0:T(8,128)(2,1)S(1)}, bf16[1024,1024]{1,0:T(8,128)(2,1)}, u32[]{:S(2)}) copy-start(bf16[1024,1024]{1,0:T(8,128)(2,1)} %get-tuple-element.20) | copy-start | bytes 6291460
  214.5 2.5 %copy-start.1 = (bf16[3072,256]{1,0:T(8,128)(2,1)S(1)}, bf16[3072,256]{1,0:T(8,128)(2,1)}, u32[]{:S(2)}) copy-start(bf16[3072,256]{1,0:T(8,128)(2,1)} %get-tuple-element.17) | copy-start | bytes 4718596
  216.9 1.9 copy-start.3
  216.9 3.0 %copy-start.4 = (bf16[256,1024]{1,0:T(8,128)(2,1)S(1)}, bf16[256,1024]{1,0:T(8,128)(2,1)}, u32[]{:S(2)}) copy-start(bf16[256,1024]{1,0:T(8,128)(2,1)} %get-tuple-element.32) | copy-start | bytes 1572868
  218.9 1.9 copy-start.2

commit v6 on v5

--- a/solution.py
+++ b/solution.py
@@ -20,6 +20,7 @@
 BF16 = jnp.bfloat16
 F32 = jnp.float32
 VMEM_LIMIT = 62 << 20
+WIDEN_STEPS = 2
 MESH_ID = pl.DeviceIdType.MESH
 
 
@@ -1130,6 +1131,35 @@
     )(x_own, dy_own, lengths, gain_attn, gain_mlp, wq, wa, wi, wo)
 
 
+def widen_kernel(*refs):
+    count = (len(refs) - 3) // 2
+    for source, target in zip(refs[:count], refs[count + 1 :]):
+        target[...] = source[...].astype(target.dtype)
+    for row, target in enumerate(refs[-2:]):
+        target[...] = refs[count][row : row + 1]
+
+
+def widen_call(arrays, kinds, gains, steps):
+    specs = [
+        pl.BlockSpec((array.shape[0] // steps, array.shape[1]), lambda step: (step, 0))
+        for array in arrays
+    ]
+    moved = sum(array.size * (array.dtype.itemsize + 4) for array in arrays)
+    return pl.pallas_call(
+        widen_kernel,
+        grid=(steps,),
+        out_shape=[
+            jax.ShapeDtypeStruct(array.shape, kind) for array, kind in zip(arrays, kinds)
+        ]
+        + [jax.ShapeDtypeStruct((1, gains.shape[1]), gains.dtype)] * 2,
+        in_specs=specs + [pl.BlockSpec(gains.shape, lambda step: (0, 0))],
+        out_specs=specs + [pl.BlockSpec((1, gains.shape[1]), lambda step: (0, 0))] * 2,
+        cost_estimate=pl.CostEstimate(flops=0, bytes_accessed=moved, transcendentals=0),
+        compiler_params=pltpu.CompilerParams(vmem_limit_bytes=VMEM_LIMIT),
+        name="widen",
+    )(*arrays, gains)
+
+
 def per_device(bits, frames, lengths, wq, wa, wi, wo, gain_attn, gain_mlp, cotangent):
     width = frames.shape[1]
     features = wa.shape[0]
@@ -1137,18 +1167,22 @@
         bits, frames, cotangent, lengths, gain_attn.reshape(1, width),
         gain_mlp.reshape(1, width), wq, wa, wi, wo,
     )
+    output, grad_frames, in_sums, out_sums, qkv_sums, wa_sums, mlp_gain, attn_gain = widen_call(
+        (output, grad_frames, in_sums, out_sums, qkv_sums, wa_sums),
+        (output.dtype,) + (F32,) * 5, gains, WIDEN_STEPS,
+    )
     if wa_sums.shape != wa.shape:
         turned = wa_sums.reshape(width // features, features, features)
         wa_sums = jnp.transpose(turned, (1, 0, 2)).reshape(features, width)
     return (
         output,
         grad_frames,
-        qkv_sums.astype(F32).reshape(3, width, features),
-        wa_sums.astype(F32),
-        in_sums.astype(F32),
-        out_sums.astype(F32),
-        gains[1],
-        gains[0],
+        qkv_sums.reshape(3, width, features),
+        wa_sums,
+        in_sums,
+        out_sums,
+        attn_gain.reshape(width),
+        mlp_gain.reshape(width),
     )
 
 

time: 222 us -> 217 us (0.977)
  other arithmetic: 9.71 us -> 0 us
  Pallas kernels: 208 us -> 216 us
  local copies, waits for them, and re-layouts: 3.22 us -> 0 us
    pallas_call x0 -> x1, Pallas kernels: none -> 8.19 us  [widen_call(): pl.pallas_call(widen_kernel, grid=(steps,), out_shape=[jax.ShapeDtypeStru...]
    convert_element_type x3 -> x0, other arithmetic: 7.78 us -> none  [the longest x1 4.22 us: per_device(): in_sums.astype(F32)]
where the time goes in v6:
time: 217 us
  Pallas kernels  216 us (100%)
    pallas_call x1, Pallas kernels, layer_call(): pl.pallas_call(functools.partial(layer_kernel, lengths.shape[1], bits), o...  208 us
    pallas_call x1, Pallas kernels, widen_call(): pl.pallas_call(widen_kernel, grid=(steps,), out_shape=[jax.ShapeDtypeStru...  8.19 us

profile of v6, /device:TPU:0, one launch (start us, length us, event | category | flops | bytes accessed | tf_op | source)
XLA Modules:
  0.0 217.2 jit_solution(1829691936651162622)
XLA Ops:
  0.6 208.2 %layer.1 = (bf16[256,1024]{1,0:T(8,128)(2,1)}, f32[256,1024]{1,0:T(8,128)}, bf16[1024,1024]{1,0:T(8,128)(2,1)}, bf16[1024,1024]{1,0:T(8,128)(2,1)}, bf16[3072,25...) custom-call(bf16[256,1024]{1,0:T(8,128)(2,1)} %x_own.1, bf16[256,1024]{1,0:T(8,128)(2,1)} %dy_own.1, ...), custom_call_target="tpu_custom_call" | custom-call | tf_op jit(solution)/shard_map/layer/pallas_call | solution.py:1115
  208.8 8.2 %widen.1 = (bf16[256,1024]{1,0:T(8,128)(2,1)}, f32[256,1024]{1,0:T(8,128)}, f32[1024,1024]{1,0:T(8,128)}, f32[1024,1024]{1,0:T(8,128)}, f32[3072,256]{1,0:T(8,12...) custom-call(bf16[256,1024]{1,0:T(8,128)(2,1)} %get-tuple-element.23.refs_0_, ...), custom_call_target="tpu_custom_call" | custom-call | bytes 22544384 | tf_op jit(solution)/shard_map/widen/pallas_call | solution.py:1148

commit v7 on v6

--- a/solution.py
+++ b/solution.py
@@ -695,9 +695,13 @@
             for number in range(chunks):
                 gather_n.take_near(number)
 
-        @pl.when((step == 1) & place.swapped)
+        @pl.when((step == 0) & place.swapped)
         def _():
             wo_parts[0].pass_on()
+
+        @pl.when((step == 2) & place.swapped)
+        def _():
+            wo_parts[1].pass_on()
 
         @pl.when(step == 2)
         def _():
@@ -706,10 +710,6 @@
                 gather_n.take_far(number)
             for number in range(chunks):
                 gather_n.take_corner(number)
-
-        @pl.when((step == 2) & place.swapped)
-        def _():
-            wo_parts[1].pass_on()
 
         hidden = dot_nn(normed_mlp[block], wi_m[...])
         square = hidden * hidden

time: 217 us -> 216 us (level)
  no operation moved by 1% of the time
where the time goes in v7:
time: 216 us
  Pallas kernels  215 us (100%)
    pallas_call x1, Pallas kernels, layer_call(): pl.pallas_call(functools.partial(layer_kernel, lengths.shape[1], bits), o...  207 us
    pallas_call x1, Pallas kernels, widen_call(): pl.pallas_call(widen_kernel, grid=(steps,), out_shape=[jax.ShapeDtypeStru...  8.19 us

profile of v7, /device:TPU:0, one launch (start us, length us, event | category | flops | bytes accessed | tf_op | source)
XLA Modules:
  0.0 216.2 jit_solution(502565394083225293)
XLA Ops:
  0.6 207.2 %layer.1 = (bf16[256,1024]{1,0:T(8,128)(2,1)}, f32[256,1024]{1,0:T(8,128)}, bf16[1024,1024]{1,0:T(8,128)(2,1)}, bf16[1024,1024]{1,0:T(8,128)(2,1)}, bf16[3072,25...) custom-call(bf16[256,1024]{1,0:T(8,128)(2,1)} %x_own.1, bf16[256,1024]{1,0:T(8,128)(2,1)} %dy_own.1, ...), custom_call_target="tpu_custom_call" | custom-call | tf_op jit(solution)/shard_map/layer/pallas_call | solution.py:1115
  207.9 8.2 %widen.1 = (bf16[256,1024]{1,0:T(8,128)(2,1)}, f32[256,1024]{1,0:T(8,128)}, f32[1024,1024]{1,0:T(8,128)}, f32[1024,1024]{1,0:T(8,128)}, f32[3072,256]{1,0:T(8,12...) custom-call(bf16[256,1024]{1,0:T(8,128)(2,1)} %get-tuple-element.23.refs_0_, ...), custom_call_target="tpu_custom_call" | custom-call | bytes 22544384 | tf_op jit(solution)/shard_map/widen/pallas_call | solution.py:1148
